TPU v7x, 768 devices: a whole 4x8x12 slice. The times are simulated.
768 devices in a mesh: ma: 48 (over x, z_lo, core), row: 16 (over z_hi, y).
Axes of the slice: x: 4, y: 8, z: 12 (z_hi: 2, z_lo: 6; z = z_hi * 6 + z_lo), core: 2. Of those that a mesh axis runs over, the one named last changes fastest.
Arguments:
- velocity: bfloat16 [3, 2, 384, 128, 384], P(None, None, 'ma', 'row'), may hold values from -6 to 6
- vorticity: bfloat16 [3, 2, 384, 128, 384], P(None, None, 'ma', 'row'), may hold values from -6 to 6
- order_table: int32 [384], replicated, may hold values from 0 to 383, as said below
- legendre_bf: bfloat16 [384, 384, 576], P('ma'), may hold values from -24 to 24, as said below
- weighted: bfloat16 [384, 384, 576], P('ma'), may hold values from -1 to 1, as said below
- inverse_operators: float32 [384, 128, 128], P('row'), may hold values from -1.5 to 1.5
Outputs:
- advanced: float32 [3, 2, 384, 384, 128], P(None, None, 'ma', 'row')
Inputs may be any that keep to these rules, and one draw needn't show every extreme that they name: `order_table`: slots 2k and 2k + 1 hold wavenumbers that add up to 383, and every wavenumber from 0 to 383 stands in exactly one slot. legendre_bf[slot, l, j] is Pbar_l^m(x_j) rounded to bfloat16, with m = order_table[slot], x_j = cos(pi (j + 0.5) / 576), s_j = sin(pi (j + 0.5) / 576), zero for l < m, Pbar_m^m = exp(-0.5 log 2 + 0.5 (lgamma(m + 1.5) - lgamma(m + 1) - lgamma(1.5)) + m log s_j) and Pbar_l^m = a (x_j Pbar_(l-1)^m - b Pbar_(l-2)^m), a = sqrt((4 l^2 - 1) / (l^2 - m^2)), b = sqrt(((l - 1)^2 - m^2) / (4 (l - 1)^2 - 1)). weighted[slot, l, j] is w_j Pbar_l^m(x_j), computed in float32 and rounded to bfloat16, with w_j = pi s_j / 576.
All inputs are finite; a program needn't handle non-finite values.
Results may differ from a plain program's by a relative error of at most 0.005.
Values may be sent and summed in bfloat16 or wider, within the bound.
No kernel may reach another device: no remote copies, remote signals or barrier semaphores. Data moves between devices by JAX's collectives and lax.ppermute only.
A program may use at most 64 MiB of HBM per device.

v0:
```python
import math

import jax
import jax.numpy as jnp
from jax import lax
from jax.sharding import PartitionSpec as P

NL = 384
NLAT = 576
NLON = 1152
NR = 128


time_step = 0.5
rotation = 2.0


def longitude_table(orders):
    points = jnp.arange(NLON, dtype=jnp.int32)
    phases = orders[:, None] * points[None, :] % NLON
    angles = phases.astype(jnp.float32) * (2.0 * math.pi / NLON)
    return jnp.stack([jnp.cos(angles), -jnp.sin(angles)]).astype(jnp.bfloat16)


def cross_terms(moving, spinning):
    spin_total = spinning[2] + rotation
    component_one = moving[1] * spin_total - moving[2] * spinning[1]
    component_two = moving[2] * spinning[0] - moving[0] * spin_total
    component_three = moving[0] * spinning[1] - moving[1] * spinning[0]
    return jnp.stack([component_one, component_two, component_three])


def per_device(velocity, vorticity, order_table, legendre_bf, weighted, inverse_operators):
    slot_count = velocity.shape[2]
    radius_count = velocity.shape[3]
    degree_count = inverse_operators.shape[0]
    own_orders = lax.dynamic_slice_in_dim(
        order_table, lax.axis_index("ma") * slot_count, slot_count
    )
    own_scale = jnp.where(own_orders == 0, 1.0, 2.0).astype(jnp.float32) / NL
    harmonics = longitude_table(order_table)

    def arrange(grid_values):
        scaled = (grid_values * own_scale[None, None, :, None, None]).astype(jnp.bfloat16)
        ordered = jnp.transpose(scaled, (0, 1, 2, 4, 3))
        return ordered.reshape(3, 2, slot_count, NLAT * radius_count)

    def synthesize(spectral):
        grid_values = jnp.einsum(
            "cpsrl,slt->cpsrt", spectral, legendre_bf, preferred_element_type=jnp.float32
        )
        return arrange(grid_values)

    def to_longitude(pieces):
        return jnp.einsum("cpsk,psn->ckn", pieces, harmonics, preferred_element_type=jnp.float32)

    velocity_grid = to_longitude(
        lax.all_to_all(synthesize(velocity), "ma", split_axis=3, concat_axis=2, tiled=True)
    )
    vorticity_grid = to_longitude(
        lax.all_to_all(synthesize(vorticity), "ma", split_axis=3, concat_axis=2, tiled=True)
    )
    products = cross_terms(velocity_grid, vorticity_grid).astype(jnp.bfloat16)
    spectral_back = jnp.einsum(
        "ckn,psn->cpsk", products, harmonics, preferred_element_type=jnp.float32
    )
    spectral_back = (NL / NLON * spectral_back).astype(jnp.bfloat16)
    pieces = lax.all_to_all(spectral_back, "ma", split_axis=2, concat_axis=3, tiled=True)
    field_count = pieces.shape[0]
    split_pieces = pieces.reshape(field_count, 2, slot_count, NLAT, radius_count)
    terms = jnp.einsum(
        "cpstr,slt->cpslr", split_pieces, weighted, preferred_element_type=jnp.float32
    )
    spec_terms = terms.reshape(field_count, 2, slot_count, NL * radius_count)
    velocity_terms = jnp.transpose(velocity.astype(jnp.float32), (0, 1, 2, 4, 3)).reshape(
        3, 2, slot_count, NL * radius_count
    )
    right_side = velocity_terms + time_step * spec_terms
    right_side = right_side.reshape(3, 2, slot_count, 1, NL * radius_count)
    operator_blocks = inverse_operators.reshape(degree_count, NR, NR // radius_count, radius_count)
    pieces = lax.all_to_all(
        right_side.astype(jnp.bfloat16), "row", split_axis=4, concat_axis=3, tiled=True
    ).astype(right_side.dtype)
    field_count = pieces.shape[0]
    columns = pieces.reshape(
        field_count, 2, slot_count, NR // radius_count, degree_count, radius_count
    )
    return jnp.einsum(
        "cpsqlr,laqr->cpsla", columns, operator_blocks, precision=lax.Precision.HIGHEST
    )


def solution(mesh):
    in_specs = (
        P(None, None, "ma", "row", None),
        P(None, None, "ma", "row", None),
        P(),
        P("ma", None, None),
        P("ma", None, None),
        P("row", None, None),
    )
    out_specs = P(None, None, "ma", "row", None)
    return jax.shard_map(
        per_device, mesh=mesh, in_specs=in_specs, out_specs=out_specs, check_vma=False
    )
```

profile of v0, /device:TPU:1, one launch (start us, length us, event | category | flops | bytes accessed | tf_op | source)
XLA Modules:
  0.0 281.1 jit_solution(11166906628631347125)
XLA Ops:
  2.0 3.0 %fusion.50 = bf16[3,2,8,576,8]{3,4,1,0,2:T(8,128)(2,1)} fusion(bf16[8,384,576]{1,2,0:T(8,128)(2,1)S(1)} %copy-done, f32[8]{0:T(128)S(1)} %fusion.70, bf16[3,2,8,8,384]{4,3,2,1,0:T(8,128)(2,1)} %param.6), kind=kOutput, calls=%fused_computation.35 | convolution fusion | flops 170311680 | bytes 4276256 | tf_op jit(solution)/shard_map/cpsrl,slt->cpsrt/dot_general | solution.py:49
  5.0 11.5 %copy.85 = bf16[3,2,8,576,8]{2,1,0,4,3:T(2,128)(2,1)} copy(bf16[3,2,8,576,8]{3,4,1,0,2:T(8,128)(2,1)} %fusion.50) | data formatting | bytes 884736 | tf_op jit(solution)/shard_map/reshape | solution.py:46
  16.5 20.6 %reshape.149 = bf16[48,2,2304]{2,1,0:T(2,128)(2,1)} reshape(bf16[4608,3,2,8]{3,2,1,0:T(2,128)(2,1)} %bitcast.118) | data formatting | bytes 884736
  37.0 16.5 %all-to-all-start = ((bf16[48,2,2304]{2,1,0:T(2,128)(2,1)}), bf16[48,2,2304]{2,1,0:T(2,128)(2,1)}, u32[]{:S(2)}, u32[]{:S(2)}) async-start(bf16[48,2,2304]{2,1,0:T(2,128)(2,1)} %reshape.149), calls=%async_computation | async-start | bytes 884736 | tf_op jit(solution)/shard_map/all_to_all | solution.py:58
  53.6 3.0 %fusion.53 = bf16[3,2,8,576,8]{3,4,1,0,2:T(8,128)(2,1)} fusion(bf16[8,384,576]{1,2,0:T(8,128)(2,1)S(1)} %copy-done, f32[8]{0:T(128)S(1)} %fusion.70, bf16[3,2,8,8,384]{4,3,2,1,0:T(8,128)(2,1)} %param.7), kind=kOutput, calls=%fused_computation.36 | convolution fusion | flops 170311680 | bytes 4276256 | tf_op jit(solution)/shard_map/cpsrl,slt->cpsrt/dot_general | solution.py:49
  56.5 11.5 %copy.88 = bf16[3,2,8,576,8]{2,1,0,4,3:T(2,128)(2,1)} copy(bf16[3,2,8,576,8]{3,4,1,0,2:T(8,128)(2,1)} %fusion.53) | data formatting | bytes 884736 | tf_op jit(solution)/shard_map/reshape | solution.py:46
  68.0 20.6 %reshape.151 = bf16[48,2,2304]{2,1,0:T(2,128)(2,1)} reshape(bf16[4608,3,2,8]{3,2,1,0:T(2,128)(2,1)} %bitcast.119) | data formatting | bytes 884736
  88.6 11.0 %all-to-all-start.1 = ((bf16[48,2,2304]{2,1,0:T(2,128)(2,1)}), bf16[48,2,2304]{2,1,0:T(2,128)(2,1)S(1)}, u32[]{:S(2)}, u32[]{:S(2)}) async-start(bf16[48,2,2304]{2,1,0:T(2,128)(2,1)} %reshape.151), calls=%async_computation.1 | async-start | bytes 884736 | tf_op jit(solution)/shard_map/all_to_all | solution.py:61
  99.6 8.0 %cosine_convert_fusion = (bf16[1,384,1152]{2,1,0:T(8,128)(2,1)S(1)}, bf16[1,384,1152]{2,1,0:T(8,128)(2,1)S(1)}) fusion(s32[384]{0:T(512)S(1)} %copy-done.5), kind=kLoop, calls=%fused_computation.19 | loop fusion | flops 5308416 | bytes 1771008 | tf_op jit(solution)/shard_map/convert.4
  107.6 22.2 %reshape.150 = bf16[4608,3,2,8]{3,2,1,0:T(2,128)(2,1)} reshape(bf16[48,2,2304]{2,1,0:T(2,128)(2,1)} %all-to-all-done) | data formatting | bytes 884736
  129.8 13.6 %copy.87 = bf16[3,2,8,48,96]{4,2,3,1,0:T(8,128)(2,1)} copy(bf16[3,2,8,48,96]{2,1,0,4,3:T(2,128)(2,1)} %bitcast.120) | data formatting | bytes 884736 | tf_op jit(solution)/shard_map/all_to_all | solution.py:58
  143.5 9.4 %reshape.152 = bf16[4608,3,2,8]{3,2,1,0:T(2,128)(2,1)} reshape(bf16[48,2,2304]{2,1,0:T(2,128)(2,1)S(1)} %all-to-all-done.1) | data formatting | bytes 884736
  152.8 13.7 %copy.90 = bf16[3,2,8,48,96]{4,2,3,1,0:T(8,128)(2,1)} copy(bf16[3,2,8,48,96]{2,1,0,4,3:T(2,128)(2,1)} %bitcast.121) | data formatting | bytes 884736 | tf_op jit(solution)/shard_map/all_to_all | solution.py:61
  166.5 1.9 convolution_bitcast_fusion.1
  170.8 34.5 %all_to_all.60 = bf16[3,2,384,96]{3,1,0,2:T(2,128)(2,1)S(1)} all-to-all(bf16[3,2,384,96]{3,1,0,2:T(2,128)(2,1)S(1)} %copy.65), channel_id=1, replica_groups=mesh['ma'=48,'row'=16] {'ma'}, dimensions={2} | all-to-all | bytes 884736 | tf_op jit(solution)/shard_map/all_to_all | solution.py:68
  206.4 8.0 %reshape.148 = bf16[3,2,8,576,8]{4,3,1,0,2:T(8,128)(2,1)} reshape(bf16[3,2,8,48,96]{4,3,1,0,2:T(8,128)(2,1)} %copy.97) | data formatting | bytes 884736 | tf_op jit(solution)/shard_map/reshape | solution.py:70
  214.4 5.7 %fusion.56 = bf16[3,2,8,384,8]{3,4,1,0,2:T(8,128)(2,1)} fusion(bf16[3,2,8,576,8]{4,3,1,0,2:T(8,128)(2,1)} %reshape.148, bf16[8,384,576]{1,2,0:T(8,128)(2,1)S(1)} %copy-done.2, bf16[3,2,8,8,384]{4,3,2,1,0:T(8,128)(2,1)} %param.6), kind=kOutput, calls=%fused_computation.37 | convolution fusion | flops 170459136 | bytes 4571136 | tf_op jit(solution)/shard_map/cpstr,slt->cpslr/dot_general | solution.py:71
  220.1 7.5 %copy.92 = bf16[3,2,8,384,8]{2,1,0,4,3:T(2,128)(2,1)} copy(bf16[3,2,8,384,8]{3,4,1,0,2:T(8,128)(2,1)} %fusion.56) | data formatting | bytes 589824 | tf_op jit(solution)/shard_map/convert_element_type | solution.py:82
  227.6 7.1 %reshape.153 = bf16[16,2,4608]{2,1,0:T(2,128)(2,1)} reshape(bf16[3072,1,3,2,8]{4,3,2,1,0:T(2,128)(2,1)} %bitcast.122) | data formatting | bytes 589824
  234.7 17.4 %all-to-all-start.3 = ((bf16[16,2,4608]{2,1,0:T(2,128)(2,1)}), bf16[16,2,4608]{2,1,0:T(2,128)(2,1)S(1)}, u32[]{:S(2)}, u32[]{:S(2)}) async-start(bf16[16,2,4608]{2,1,0:T(2,128)(2,1)} %reshape.153), calls=%async_computation.3 | async-start | bytes 589824 | tf_op jit(solution)/shard_map/all_to_all | solution.py:81
  252.1 1.6 copy.72
  253.7 13.0 %all-to-all-done.3 = bf16[16,2,4608]{2,1,0:T(2,128)(2,1)S(1)} async-done(((bf16[16,2,4608]{2,1,0:T(2,128)(2,1)}), bf16[16,2,4608]{2,1,0:T(2,128)(2,1)S(1)}, u32[]{:S(2)}, u32[]{:S(2)}) %all-to-all-start.3) | async-done | bytes 294944 | tf_op jit(solution)/shard_map/all_to_all | solution.py:81
  266.7 6.6 %reshape.154 = bf16[3072,1,3,2,8]{4,3,2,1,0:T(2,128)(2,1)} reshape(bf16[16,2,4608]{2,1,0:T(2,128)(2,1)S(1)} %all-to-all-done.3) | data formatting | bytes 589824
  273.3 6.8 %fusion.45 = f32[3,2,8,24,128]{4,2,1,0,3:T(8,128)S(1)} fusion(f32[24,128,128]{1,2,0:T(8,128)} %copy.72, bf16[3,2,8,16,24,8]{2,1,0,5,4,3:T(2,128)(2,1)} %bitcast.123), kind=kOutput, calls=%fused_computation.34 | convolution fusion | flops 226492416 | bytes 2457600 | tf_op jit(solution)/shard_map/cpsqlr,laqr->cpsla/dot_general | solution.py:88
  (22 shorter events, 6.4 us)
Async XLA Ops:
  0.0 2.0 copy-start
  37.0 51.6 %all-to-all-start = ((bf16[48,2,2304]{2,1,0:T(2,128)(2,1)}), bf16[48,2,2304]{2,1,0:T(2,128)(2,1)}, u32[]{:S(2)}, u32[]{:S(2)}) async-start(bf16[48,2,2304]{2,1,0:T(2,128)(2,1)} %reshape.149), calls=%async_computation | async-start | bytes 884736 | tf_op jit(solution)/shard_map/all_to_all | solution.py:58
  68.0 31.6 %copy-start.5 = (s32[384]{0:T(512)S(1)}, s32[384]{0:T(512)}, u32[]{:S(2)}) copy-start(s32[384]{0:T(512)} %param.8) | copy-start | bytes 4612
  88.6 54.9 %all-to-all-start.1 = ((bf16[48,2,2304]{2,1,0:T(2,128)(2,1)}), bf16[48,2,2304]{2,1,0:T(2,128)(2,1)S(1)}, u32[]{:S(2)}, u32[]{:S(2)}) async-start(bf16[48,2,2304]{2,1,0:T(2,128)(2,1)} %reshape.151), calls=%async_computation.1 | async-start | bytes 884736 | tf_op jit(solution)/shard_map/all_to_all | solution.py:61
  166.5 1.9 copy-start.3
  206.4 8.0 %copy-start.2 = (bf16[8,384,576]{1,2,0:T(8,128)(2,1)S(1)}, bf16[8,384,576]{1,2,0:T(8,128)(2,1)}, u32[]{:S(2)}) copy-start(bf16[8,384,576]{1,2,0:T(8,128)(2,1)} %param.10) | copy-start | bytes 10616836
  227.6 24.4 %copy-start.4 = (f32[24,128,128]{2,1,0:T(8,128)S(1)}, f32[24,128,128]{2,1,0:T(8,128)}, u32[]{:S(2)}) copy-start(f32[24,128,128]{2,1,0:T(8,128)} %param.11) | copy-start | bytes 4718596
  234.7 32.0 %all-to-all-start.3 = ((bf16[16,2,4608]{2,1,0:T(2,128)(2,1)}), bf16[16,2,4608]{2,1,0:T(2,128)(2,1)S(1)}, u32[]{:S(2)}, u32[]{:S(2)}) async-start(bf16[16,2,4608]{2,1,0:T(2,128)(2,1)} %reshape.153), calls=%async_computation.3 | async-start | bytes 589824 | tf_op jit(solution)/shard_map/all_to_all | solution.py:81
  273.3 7.8 %copy-start.1 = (bf16[8,384,576]{1,2,0:T(8,128)(2,1)S(1)}, bf16[8,384,576]{1,2,0:T(8,128)(2,1)}, u32[]{:S(2)}) copy-start(bf16[8,384,576]{1,2,0:T(8,128)(2,1)} %param.9) | copy-start | bytes 10616836
where the time goes:
time: 286 us; the launch traced here: 281 us
  local copies, waits for them, and re-layouts  157 us (55%)
  starting transfers between devices  44.9 us (16%)
  blocking collectives  34.5 us (12%)
  matrix products  22 us (8%)
  waiting for transfers between devices  13 us (5%)
  other arithmetic  9.19 us (3%)
    unnamed x19, local copies, waits for them, and re-layouts  89.1 us
    all_to_all x1, blocking collectives, per_device(): lax.all_to_all(spectral_back, 'ma', split_axis=2, concat_axis=3, tiled=True)  34.5 us
    reshape x2, local copies, waits for them, and re-layouts, arrange(): return ordered.reshape(3, 2, slot_count, NLAT * radius_count)  23 us
    all_to_all x1, starting transfers between devices, per_device(): lax.all_to_all(right_side.astype(jnp.bfloat16), 'row', split_axis=4, conc...  17.4 us
    all_to_all x1, starting transfers between devices, per_device(): lax.all_to_all(synthesize(velocity), 'ma', split_axis=3, concat_axis=2, t...  16.5 us
    all_to_all x1, local copies, waits for them, and re-layouts, per_device(): lax.all_to_all(synthesize(vorticity), 'ma', split_axis=3, concat_axis=2,...  13.7 us
    all_to_all x1, local copies, waits for them, and re-layouts, per_device(): lax.all_to_all(synthesize(velocity), 'ma', split_axis=3, concat_axis=2, t...  13.6 us
    all_to_all x1, waiting for transfers between devices, per_device(): lax.all_to_all(right_side.astype(jnp.bfloat16), 'row', split_axis=4, conc...  13 us
  transfers between devices with their start and end apart: 3, of which 1 were waited for; matrix products, arithmetic and copies ran while one was open for 29% of the time, Pallas kernels for 0%

commit v1 on v0

v1 whole, which is shorter than its diff:
```python
import functools
import math

import jax
import jax.numpy as jnp
from jax import lax
from jax.experimental import pallas as pl
from jax.experimental.pallas import tpu as pltpu
from jax.sharding import PartitionSpec as P

NL = 384
NLAT = 576
NLON = 1152
NR = 128
LANES = 128


time_step = 0.5
rotation = 2.0

NT_DIMS = (((1,), (1,)), ((), ()))


def dot(left, right, dims=(((1,), (0,)), ((), ()))):
    return lax.dot_general(left, right, dims, preferred_element_type=jnp.float32)


def angle_parts(orders, steps):
    phases = orders[:, None] * steps[None, :] % NLON
    angles = phases.astype(jnp.float32) * (2.0 * math.pi / NLON)
    return jnp.cos(angles), jnp.sin(angles)


def harmonics_kernel(coarse_cos, coarse_sin, fine_cos, fine_sin, table):
    cos_b = fine_cos[...]
    sin_b = fine_sin[...]
    for block in range(NLON // LANES):
        cos_a = coarse_cos[:, block : block + 1]
        sin_a = coarse_sin[:, block : block + 1]
        lanes = pl.ds(block * LANES, LANES)
        table[0, :, lanes] = (cos_a * cos_b - sin_a * sin_b).astype(jnp.bfloat16)
        table[1, :, lanes] = (-(sin_a * cos_b + cos_a * sin_b)).astype(jnp.bfloat16)


def synthesis_kernel(groups, width, orders, velocity, vorticity, legendre, out, stage, rows, blocks):
    slot = pl.program_id(0)
    radii = velocity.shape[1]
    slots = orders.shape[0]
    own = jnp.where(orders[slot] == 0, 1.0, 2.0).astype(jnp.float32) / NL
    for index, field in enumerate((velocity, vorticity)):
        half = field.shape[0] * radii
        spectral = field[...].astype(jnp.float32).reshape(half, NL).astype(jnp.bfloat16)
        stage[index * half : (index + 1) * half, :] = dot(spectral, legendre[0], NT_DIMS) * own
    for group in range(groups):
        for component in range(6):
            for part in range(2):
                source = (component * 2 + part) * radii
                target = (part * 6 + component) * width
                rows[group, :, target : target + width] = stage[
                    source : source + radii, group * width : (group + 1) * width
                ]
        for tile in range(blocks.shape[0]):
            lanes = slice(tile * LANES, (tile + 1) * LANES)
            blocks[tile, pl.ds(group * radii * slots + slot, radii, stride=slots), :] = rows[group, :, lanes]

    @pl.when(slot == slots - 1)
    def finish():
        for tile in range(blocks.shape[0]):
            out[:, tile * LANES : (tile + 1) * LANES] = blocks[tile].astype(jnp.bfloat16)


def longitude_kernel(width, received, table, out, stage):
    points = 6 * width
    turned = received[...].astype(jnp.float32).T.astype(jnp.bfloat16)
    grid = dot(turned[:points], table[0]) + dot(turned[points:], table[1])
    u = [grid[c * width : (c + 1) * width] for c in range(3)]
    w = [grid[(3 + c) * width : (4 + c) * width] for c in range(3)]
    spin = w[2] + rotation
    products = jnp.concatenate(
        [
            u[1] * spin - u[2] * w[1],
            u[2] * w[0] - u[0] * spin,
            u[0] * w[1] - u[1] * w[0],
        ],
        axis=0,
    ).astype(jnp.bfloat16)
    for part in range(2):
        back = dot(table[part], products, NT_DIMS) * (NL / NLON)
        stage[:, part * 3 * width : (part + 1) * 3 * width] = back
    out[...] = stage[...].astype(jnp.bfloat16)


def analysis_kernel(groups, width, degrees, received, velocity, weighted, out, whole, rows, stage, side, blocks):
    slots = weighted.shape[0]
    radii = velocity.shape[2]
    owners = NL // degrees
    lanes = 6 * width
    for tile in range(whole.shape[0]):
        size = min(LANES, lanes - tile * LANES)
        whole[tile, :, :size] = received[:, tile * LANES : tile * LANES + size].astype(jnp.float32)
    for slot in range(slots):
        for group in range(groups):
            for tile in range(whole.shape[0]):
                rows[slot, group, :, tile * LANES : (tile + 1) * LANES] = whole[
                    tile, pl.ds(group * radii * slots + slot, radii, stride=slots), :
                ]
            for component in range(3):
                for part in range(2):
                    source = (part * 3 + component) * width
                    target = (component * 2 + part) * radii
                    stage[slot, target : target + radii, group * width : (group + 1) * width] = rows[
                        slot, group, :, source : source + width
                    ]
        terms = dot(stage[slot].astype(jnp.bfloat16), weighted[slot])
        known = velocity[:, slot].astype(jnp.float32).reshape(6 * radii, NL)
        side[slot] = known + time_step * terms
        for owner in range(owners):
            for field in range(6):
                target = (field * slots + slot) * degrees
                blocks[owner * radii : (owner + 1) * radii, target : target + degrees] = side[
                    slot, field * radii : (field + 1) * radii, owner * degrees : (owner + 1) * degrees
                ]
    out[...] = blocks[...].astype(jnp.bfloat16)


def solve_kernel(received, operators, out, turned):
    degrees = operators.shape[0]
    count = received.shape[1] // degrees
    turned[...] = received[...].astype(jnp.float32).T
    for degree in range(degrees):
        rows = turned[pl.ds(degree, count, stride=degrees), :].astype(jnp.bfloat16)
        operator = operators[degree]
        high = operator.astype(jnp.bfloat16)
        low = (operator - high.astype(jnp.float32)).astype(jnp.bfloat16)
        out[pl.ds(degree, count, stride=degrees), :] = dot(rows, high, NT_DIMS) + dot(rows, low, NT_DIMS)


def per_device(velocity, vorticity, order_table, legendre_bf, weighted, inverse_operators):
    slots = velocity.shape[2]
    radii = velocity.shape[3]
    degrees = inverse_operators.shape[0]
    members = NL // slots
    owners = NL // degrees
    groups = members // radii
    width = NLAT // groups
    f32, bf16 = jnp.float32, jnp.bfloat16
    vmem = pl.BlockSpec(memory_space=pltpu.VMEM)

    own_orders = lax.dynamic_slice_in_dim(order_table, lax.axis_index("ma") * slots, slots)
    velocity_rows = velocity.reshape(6, slots, radii, NL)
    vorticity_rows = vorticity.reshape(6, slots, radii, NL)
    legendre_rows = jnp.swapaxes(legendre_bf, 1, 2)
    weighted_rows = jnp.swapaxes(weighted, 1, 2)

    field_spec = pl.BlockSpec((6, None, radii, NL), lambda s: (0, s, 0, 0))
    sums = pl.pallas_call(
        functools.partial(synthesis_kernel, groups, width),
        grid=(slots,),
        in_specs=[
            pl.BlockSpec(memory_space=pltpu.SMEM),
            field_spec,
            field_spec,
            pl.BlockSpec((1, NLAT, NL), lambda s: (s, 0, 0)),
        ],
        out_specs=pl.BlockSpec((members * slots, 12 * width), lambda s: (0, 0)),
        out_shape=jax.ShapeDtypeStruct((members * slots, 12 * width), bf16),
        scratch_shapes=[
            pltpu.VMEM((12 * radii, NLAT), f32),
            pltpu.VMEM((groups, radii, 12 * width), f32),
            pltpu.VMEM((12 * width // LANES, members * slots, LANES), f32),
        ],
        name="synthesis",
    )(own_orders, velocity_rows, vorticity_rows, legendre_rows)
    pieces = lax.all_to_all(
        sums.reshape(members, slots, 12 * width), "ma", split_axis=0, concat_axis=0, tiled=True
    ).reshape(members * slots, 12 * width)

    coarse_cos, coarse_sin = angle_parts(order_table, LANES * jnp.arange(LANES, dtype=jnp.int32) % NLON)
    fine_cos, fine_sin = angle_parts(order_table, jnp.arange(LANES, dtype=jnp.int32))
    table = pl.pallas_call(
        harmonics_kernel,
        in_specs=[vmem] * 4,
        out_specs=vmem,
        out_shape=jax.ShapeDtypeStruct((2, NL, NLON), bf16),
        cost_estimate=pl.CostEstimate(flops=6 * NL * NLON, bytes_accessed=8 * NL * NLON, transcendentals=0),
        name="harmonics",
    )(coarse_cos, coarse_sin, fine_cos, fine_sin)

    tendency = pl.pallas_call(
        functools.partial(longitude_kernel, width),
        in_specs=[vmem] * 2,
        out_specs=vmem,
        out_shape=jax.ShapeDtypeStruct((NL, 6 * width), bf16),
        scratch_shapes=[pltpu.VMEM((NL, 6 * width), f32)],
        name="longitude",
    )(pieces, table)
    pieces = lax.all_to_all(
        tendency.reshape(members, slots, 6 * width), "ma", split_axis=0, concat_axis=0, tiled=True
    ).reshape(members * slots, 6 * width)

    lanes = 6 * slots * degrees
    tiles = pl.cdiv(6 * width, LANES)
    sides = pl.pallas_call(
        functools.partial(analysis_kernel, groups, width, degrees),
        in_specs=[vmem] * 3,
        out_specs=vmem,
        out_shape=jax.ShapeDtypeStruct((owners * radii, lanes), bf16),
        scratch_shapes=[
            pltpu.VMEM((tiles, members * slots, LANES), f32),
            pltpu.VMEM((slots, groups, radii, tiles * LANES), f32),
            pltpu.VMEM((slots, 6 * radii, NLAT), f32),
            pltpu.VMEM((slots, 6 * radii, NL), f32),
            pltpu.VMEM((owners * radii, lanes), f32),
        ],
        name="analysis",
    )(pieces, velocity_rows, weighted_rows)
    columns = lax.all_to_all(
        sides.reshape(owners, radii, lanes), "row", split_axis=0, concat_axis=0, tiled=True
    ).reshape(NR, lanes)

    advanced = pl.pallas_call(
        solve_kernel,
        in_specs=[vmem] * 2,
        out_specs=vmem,
        out_shape=jax.ShapeDtypeStruct((lanes, NR), f32),
        scratch_shapes=[pltpu.VMEM((lanes, NR), f32)],
        name="solve",
    )(columns, inverse_operators)
    return advanced.reshape(3, 2, slots, degrees, NR)


def solution(mesh):
    in_specs = (
        P(None, None, "ma", "row", None),
        P(None, None, "ma", "row", None),
        P(),
        P("ma", None, None),
        P("ma", None, None),
        P("row", None, None),
    )
    out_specs = P(None, None, "ma", "row", None)
    return jax.shard_map(
        per_device, mesh=mesh, in_specs=in_specs, out_specs=out_specs, check_vma=False
    )
```

time: 286 us -> 136 us (0.48); the launches traced: 281 us -> 135 us
  local copies, waits for them, and re-layouts: 157 us -> 2.26 us
  starting transfers between devices: 44.9 us -> 16.4 us
  Pallas kernels: 0 us -> 26.3 us
  blocking collectives: 34.5 us -> 58.7 us
  matrix products: 22 us -> 0 us
  waiting for transfers between devices: 13 us -> 28.7 us
  other arithmetic: 9.19 us -> 2.59 us
    unnamed x19 -> x4, local copies, waits for them, and re-layouts: 89.1 us -> 0.93 us
    reshape x4 -> x0, local copies, waits for them, and re-layouts: 31.9 us -> none  [the longest x2 23 us: arrange(): return ordered.reshape(3, 2, slot_count, NLAT * radius_count)]
    all_to_all x3 -> x1, starting transfers between devices: 44.9 us -> 16.4 us  [per_device(): lax.all_to_all(sums.reshape(members, slots, 12 * width), 'ma', split_axis...]
    all_to_all x3 -> x0, local copies, waits for them, and re-layouts: 27.4 us -> none  [the longest x1 13.7 us: per_device(): lax.all_to_all(synthesize(vorticity), 'ma', split_axis=3, concat_axis=2,...]
    pallas_call x0 -> x5, Pallas kernels: none -> 26.3 us  [the longest x1 7.97 us: per_device(): pl.pallas_call(functools.partial(synthesis_kernel, groups, width), grid=(...]
    all_to_all x1 -> x2, blocking collectives: 34.5 us -> 58.7 us  [the longest x1 31.2 us: per_device(): lax.all_to_all(sides.reshape(owners, radii, lanes), 'row', split_axis=0,...]
    dot_general x7 -> x0, matrix products: 22 us -> none  [the longest x1 6.82 us: per_device(): jnp.einsum('cpsqlr,laqr->cpsla', columns, operator_blocks, precision=lax....]
    all_to_all x3 -> x1, waiting for transfers between devices: 13 us -> 28.7 us  [per_device(): lax.all_to_all(sums.reshape(members, slots, 12 * width), 'ma', split_axis...]
  transfers between devices with their start and end apart: 3 -> 1, of which waited for: 1 -> 1; matrix products, arithmetic and copies ran while one was open for 29% -> 2% of each run, Pallas kernels for 0% -> 3%
where the time goes in v1:
time: 136 us; the launch traced here: 135 us
  blocking collectives  58.7 us (43%)
  waiting for transfers between devices  28.7 us (21%)
  Pallas kernels  26.3 us (19%)
  starting transfers between devices  16.4 us (12%)
  other arithmetic  2.59 us (2%)
  local copies, waits for them, and re-layouts  2.26 us (2%)
    all_to_all x1, blocking collectives, per_device(): lax.all_to_all(sides.reshape(owners, radii, lanes), 'row', split_axis=0,...  31.2 us
    all_to_all x1, waiting for transfers between devices, per_device(): lax.all_to_all(sums.reshape(members, slots, 12 * width), 'ma', split_axis...  28.7 us
    all_to_all x1, blocking collectives, per_device(): lax.all_to_all(tendency.reshape(members, slots, 6 * width), 'ma', split_a...  27.5 us
    all_to_all x1, starting transfers between devices, per_device(): lax.all_to_all(sums.reshape(members, slots, 12 * width), 'ma', split_axis...  16.4 us
    pallas_call x1, Pallas kernels, per_device(): pl.pallas_call(functools.partial(synthesis_kernel, groups, width), grid=(...  7.97 us
    pallas_call x1, Pallas kernels, per_device(): pl.pallas_call(functools.partial(analysis_kernel, groups, width, degrees)...  5.79 us
    pallas_call x1, Pallas kernels, per_device(): pl.pallas_call(functools.partial(longitude_kernel, width), in_specs=[vmem...  5.39 us
    pallas_call x1, Pallas kernels, per_device(): pl.pallas_call(solve_kernel, in_specs=[vmem] * 2, out_specs=vmem, out_sha...  3.64 us
  transfers between devices with their start and end apart: 1, of which 1 were waited for; matrix products, arithmetic and copies ran while one was open for 2% of the time, Pallas kernels for 3%

profile of v1, /device:TPU:1, one launch (start us, length us, event | category | flops | bytes accessed | tf_op | source)
XLA Modules:
  0.0 135.0 jit_solution(3726932177783138113)
XLA Ops:
  0.0 0.0 copy-start.1
  0.0 1.3 dynamic_slice.3.orders
  1.3 8.0 %synthesis.1 = bf16[384,1152]{1,0:T(8,128)(2,1)} custom-call(s32[8]{0:T(128)} %dynamic_slice.3.orders, bf16[6,8,8,384]{3,2,1,0:T(8,128)(2,1)} %bitcast.19, bf16[6,8,8,384]{3,2,1,0:T(8,128)(2,1)} %bitcast.21, bf16[8,576,384]{2,1,0:T(8,128)(2,1)} %bitcast.13), custom_call_target="tpu_custom_call" | custom-call | tf_op jit(solution)/shard_map/synthesis/pallas_call | solution.py:156
  9.3 16.4 %all-to-all-start = ((bf16[48,8,1152]{2,1,0:T(8,128)(2,1)}), bf16[48,8,1152]{2,1,0:T(8,128)(2,1)S(1)}, u32[]{:S(2)}, u32[]{:S(2)}) async-start(bf16[48,8,1152]{2,1,0:T(8,128)(2,1)} %bitcast.14), calls=%async_computation | async-start | bytes 1769472 | tf_op jit(solution)/shard_map/all_to_all | solution.py:174
  25.7 0.0 copy-done.1
  25.8 2.6 %fusion.10 = (f32[384,128]{1,0:T(8,128)}, f32[384,128]{1,0:T(8,128)}, f32[384,128]{1,0:T(8,128)}, f32[384,128]{1,0:T(8,128)}) fusion(s32[128]{0:T(128)S(1)} %and_select_fusion, s32[384]{0:T(512)S(1)} %copy-done.1), kind=kLoop, calls=%fused_computation.14 | loop fusion | flops 884736 | bytes 788480 | tf_op jit(solution)/shard_map/sin | solution.py:31
  28.3 3.5 %harmonics.1.table = bf16[2,384,1152]{2,1,0:T(8,128)(2,1)} custom-call(f32[384,128]{1,0:T(8,128)} %get-tuple-element.6.coarse_cos, f32[384,128]{1,0:T(8,128)} %get-tuple-element.5.coarse_sin, f32[384,128]{1,0:T(8,128)} %get-tuple-element.8.fine_cos, f32[384,128]{1,0:T(8,128)} %get-tuple-element.7.fine_sin), custom_call_target="tpu_custom_call" | custom-call | flops 2654208 | bytes 3538944 | tf_op jit(solution)/shard_map/harmonics/pallas_call | solution.py:180
  31.8 28.7 %all-to-all-done = bf16[48,8,1152]{2,1,0:T(8,128)(2,1)S(1)} async-done(((bf16[48,8,1152]{2,1,0:T(8,128)(2,1)}), bf16[48,8,1152]{2,1,0:T(8,128)(2,1)S(1)}, u32[]{:S(2)}, u32[]{:S(2)}) %all-to-all-start) | async-done | bytes 884768 | tf_op jit(solution)/shard_map/all_to_all | solution.py:174
  60.6 0.0 copy-start
  60.6 0.9 copy-done
  61.5 5.4 %longitude.1 = bf16[384,576]{1,0:T(8,128)(2,1)} custom-call(bf16[384,1152]{1,0:T(8,128)(2,1)} %bitcast.11, bf16[2,384,1152]{2,1,0:T(8,128)(2,1)} %harmonics.1.table), custom_call_target="tpu_custom_call" | custom-call | tf_op jit(solution)/shard_map/longitude/pallas_call | solution.py:189
  66.9 27.5 %all_to_all.15 = bf16[48,8,576]{2,1,0:T(8,128)(2,1)} all-to-all(bf16[48,8,576]{2,1,0:T(8,128)(2,1)} %bitcast.15), channel_id=1, replica_groups=mesh['ma'=48,'row'=16] {'ma'}, dimensions={0} | all-to-all | bytes 884736 | tf_op jit(solution)/shard_map/all_to_all | solution.py:197
  94.4 5.8 %analysis.1 = bf16[128,1152]{1,0:T(8,128)(2,1)} custom-call(bf16[384,576]{1,0:T(8,128)(2,1)} %bitcast.16, bf16[6,8,8,384]{3,2,1,0:T(8,128)(2,1)} %bitcast.20, bf16[8,576,384]{2,1,0:T(8,128)(2,1)} %bitcast.12), custom_call_target="tpu_custom_call" | custom-call | tf_op jit(solution)/shard_map/analysis/pallas_call | solution.py:203
  100.2 31.2 %all_to_all.16 = bf16[16,8,1152]{2,1,0:T(8,128)(2,1)} all-to-all(bf16[16,8,1152]{2,1,0:T(8,128)(2,1)} %bitcast.17), channel_id=1, replica_groups=mesh['ma'=48,'row'=16] {'row'}, dimensions={0} | all-to-all | bytes 589824 | tf_op jit(solution)/shard_map/all_to_all | solution.py:217
  131.4 3.6 %solve.1 = f32[1152,128]{1,0:T(8,128)} custom-call(bf16[128,1152]{1,0:T(8,128)(2,1)} %bitcast.18, f32[24,128,128]{2,1,0:T(8,128)} %operators.1), custom_call_target="tpu_custom_call" | custom-call | tf_op jit(solution)/shard_map/solve/pallas_call | solution.py:221
  (1 shorter events, 0.0 us)
Async XLA Ops:
  0.0 25.7 %copy-start.1 = (s32[384]{0:T(512)S(1)}, s32[384]{0:T(512)}, u32[]{:S(2)}) copy-start(s32[384]{0:T(512)} %param.8) | copy-start | bytes 4612
  9.3 51.3 %all-to-all-start = ((bf16[48,8,1152]{2,1,0:T(8,128)(2,1)}), bf16[48,8,1152]{2,1,0:T(8,128)(2,1)S(1)}, u32[]{:S(2)}, u32[]{:S(2)}) async-start(bf16[48,8,1152]{2,1,0:T(8,128)(2,1)} %bitcast.14), calls=%async_computation | async-start | bytes 1769472 | tf_op jit(solution)/shard_map/all_to_all | solution.py:174
  60.6 0.9 copy-start

commit v2 on v1

v2 whole, which is shorter than its diff:
```python
import functools
import math

import jax
import jax.numpy as jnp
from jax import lax
from jax.experimental import pallas as pl
from jax.experimental.pallas import tpu as pltpu
from jax.sharding import PartitionSpec as P

NL = 384
NLAT = 576
NLON = 1152
NR = 128
LANES = 128


time_step = 0.5
rotation = 2.0

NT_DIMS = (((1,), (1,)), ((), ()))


def dot(left, right, dims=(((1,), (0,)), ((), ()))):
    return lax.dot_general(left, right, dims, preferred_element_type=jnp.float32)


def angle_parts(orders, steps):
    phases = orders[:, None] * steps[None, :] % NLON
    angles = phases.astype(jnp.float32) * (2.0 * math.pi / NLON)
    return jnp.cos(angles), jnp.sin(angles)


def harmonics_kernel(coarse_cos, coarse_sin, fine_cos, fine_sin, table):
    cos_b = fine_cos[...]
    sin_b = fine_sin[...]
    for block in range(NLON // LANES):
        cos_a = coarse_cos[:, block : block + 1]
        sin_a = coarse_sin[:, block : block + 1]
        lanes = pl.ds(block * LANES, LANES)
        table[0, :, lanes] = (cos_a * cos_b - sin_a * sin_b).astype(jnp.bfloat16)
        table[1, :, lanes] = (-(sin_a * cos_b + cos_a * sin_b)).astype(jnp.bfloat16)


def lane_index():
    return lax.broadcasted_iota(jnp.int32, (8, LANES), 1)


def joined(pieces, width, tile):
    start = tile * LANES
    lanes = lane_index()
    result = None
    for index in range(start // width, min(len(pieces), (start + LANES - 1) // width + 1)):
        offset = index * width - start
        moved = pieces[index]
        if offset % LANES:
            moved = pltpu.roll(moved, offset % LANES, 1)
        result = moved if result is None else jnp.where(lanes >= offset, moved, result)
    return result


def parted(tiles, width, index):
    tile, offset = divmod(index * width, LANES)
    piece = tiles[tile]
    if offset + width > LANES:
        piece = jnp.where(lane_index() >= offset, piece, tiles[tile + 1])
    if offset:
        piece = pltpu.roll(piece, LANES - offset, 1)
    return piece


def synthesis_kernel(groups, width, orders, velocity, vorticity, legendre, out, stage):
    slot = pl.program_id(0)
    slots = orders.shape[0]
    radii = velocity.shape[1]
    count = 12 * radii
    own = jnp.where(orders[slot] == 0, 1.0, 2.0).astype(jnp.float32) / NL
    spectral = jnp.concatenate([velocity[...], vorticity[...]], axis=0)
    spectral = spectral.astype(jnp.float32).reshape(count, NL).astype(jnp.bfloat16)
    rows = pl.ds(pl.multiple_of(slot * count, 8), count)
    for group in range(groups):
        part = dot(spectral, legendre[0, group * width : (group + 1) * width, :], NT_DIMS)
        stage[group, rows, :width] = part * own

    @pl.when(slot == slots - 1)
    def finish():
        def receiver(index, carry):
            group, radius = index // radii, index % radii
            pieces = [
                stage[group, pl.ds((component * 2 + part) * radii + radius, slots, stride=count), :]
                for part in range(2)
                for component in range(6)
            ]
            target = pl.ds(pl.multiple_of(index * slots, 8), slots)
            for tile in range(12 * width // LANES):
                lanes = slice(tile * LANES, (tile + 1) * LANES)
                out[target, lanes] = joined(pieces, width, tile).astype(jnp.bfloat16)
            return carry

        lax.fori_loop(0, groups * radii, receiver, 0, unroll=4)


def longitude_kernel(width, received, table, out, stage):
    points = 6 * width
    turned = received[...].astype(jnp.float32).T.astype(jnp.bfloat16)
    grid = dot(turned[:points], table[0]) + dot(turned[points:], table[1])
    u = [grid[c * width : (c + 1) * width] for c in range(3)]
    w = [grid[(3 + c) * width : (4 + c) * width] for c in range(3)]
    spin = w[2] + rotation
    products = jnp.concatenate(
        [
            u[1] * spin - u[2] * w[1],
            u[2] * w[0] - u[0] * spin,
            u[0] * w[1] - u[1] * w[0],
        ],
        axis=0,
    ).astype(jnp.bfloat16)
    for part in range(2):
        back = dot(table[part], products, NT_DIMS) * (NL / NLON)
        stage[:, part * 3 * width : (part + 1) * 3 * width] = back
    out[...] = stage[...].astype(jnp.bfloat16)


def analysis_kernel(groups, width, received, velocity, weighted, out, whole, side):
    slots = weighted.shape[0]
    radii = velocity.shape[2]
    tiles = whole.shape[0]
    for tile in range(tiles):
        size = min(LANES, 6 * width - tile * LANES)
        whole[tile, :, :size] = received[:, tile * LANES : tile * LANES + size].astype(jnp.float32)
    for slot in range(slots):
        terms = None
        for group in range(groups):
            source = pl.ds(group * radii * slots + slot, radii, stride=slots)
            parts = [whole[tile, source, :] for tile in range(tiles)]
            fields = [parted(parts, width, part * 3 + component) for component in range(3) for part in range(2)]
            block = jnp.concatenate(fields, axis=0)[:, :width].astype(jnp.bfloat16)
            term = dot(block, weighted[slot, group * width : (group + 1) * width, :])
            terms = term if terms is None else terms + term
        known = velocity[:, slot].astype(jnp.float32).reshape(6 * radii, NL)
        right_side = known + time_step * terms
        for field in range(6):
            for tile in range(NL // LANES):
                side[tile, pl.ds(field * slots + slot, radii, stride=6 * slots), :] = right_side[
                    field * radii : (field + 1) * radii, tile * LANES : (tile + 1) * LANES
                ]
    for tile in range(NL // LANES):
        out[tile * LANES : (tile + 1) * LANES, :] = side[tile].T.astype(jnp.bfloat16)


def solve_kernel(received, operators, out, whole, square):
    degrees = operators.shape[0]
    owners = received.shape[0] // degrees
    radii = NR // owners
    count = received.shape[1] // radii
    tiles = whole.shape[0]
    for tile in range(tiles):
        whole[tile] = received[:, tile * LANES : (tile + 1) * LANES].astype(jnp.float32)

    def solve(degree, carry):
        for half in range(owners // 8):
            source = pl.ds(half * 8 * degrees + degree, 8, stride=degrees)
            parts = [whole[tile, source, :] for tile in range(tiles)]
            for radius in range(radii):
                target = pl.ds(half * 8 * radii + radius, 8, stride=radii)
                square[degree, target, :] = parted(parts, count, radius)
        columns = square[degree].T[:count].astype(jnp.bfloat16)
        operator = operators[degree]
        high = operator.astype(jnp.bfloat16)
        low = (operator - high.astype(jnp.float32)).astype(jnp.bfloat16)
        out[pl.ds(degree, count, stride=degrees), :] = dot(columns, high, NT_DIMS) + dot(columns, low, NT_DIMS)
        return carry

    lax.fori_loop(0, degrees, solve, 0, unroll=4)


def per_device(velocity, vorticity, order_table, legendre_bf, weighted, inverse_operators):
    slots = velocity.shape[2]
    radii = velocity.shape[3]
    degrees = inverse_operators.shape[0]
    members = NL // slots
    owners = NL // degrees
    groups = members // radii
    width = NLAT // groups
    f32, bf16 = jnp.float32, jnp.bfloat16
    vmem = pl.BlockSpec(memory_space=pltpu.VMEM)
    params = pltpu.CompilerParams(vmem_limit_bytes=24 * 2**20)

    own_orders = lax.dynamic_slice_in_dim(order_table, lax.axis_index("ma") * slots, slots)
    velocity_rows = velocity.reshape(6, slots, radii, NL)
    vorticity_rows = vorticity.reshape(6, slots, radii, NL)
    legendre_rows = jnp.swapaxes(legendre_bf, 1, 2)
    weighted_rows = jnp.swapaxes(weighted, 1, 2)

    field_spec = pl.BlockSpec((6, None, radii, NL), lambda s: (0, s, 0, 0))
    sums = pl.pallas_call(
        functools.partial(synthesis_kernel, groups, width),
        grid=(slots,),
        in_specs=[
            pl.BlockSpec(memory_space=pltpu.SMEM),
            field_spec,
            field_spec,
            pl.BlockSpec((1, NLAT, NL), lambda s: (s, 0, 0)),
        ],
        out_specs=pl.BlockSpec((members * slots, 12 * width), lambda s: (0, 0)),
        out_shape=jax.ShapeDtypeStruct((members * slots, 12 * width), bf16),
        scratch_shapes=[
            pltpu.VMEM((groups, slots * 12 * radii, LANES), f32),
        ],
        name="synthesis",
    )(own_orders, velocity_rows, vorticity_rows, legendre_rows)
    pieces = lax.all_to_all(
        sums.reshape(members, slots, 12 * width), "ma", split_axis=0, concat_axis=0, tiled=True
    ).reshape(members * slots, 12 * width)

    coarse_cos, coarse_sin = angle_parts(order_table, LANES * jnp.arange(LANES, dtype=jnp.int32) % NLON)
    fine_cos, fine_sin = angle_parts(order_table, jnp.arange(LANES, dtype=jnp.int32))
    table = pl.pallas_call(
        harmonics_kernel,
        in_specs=[vmem] * 4,
        out_specs=vmem,
        out_shape=jax.ShapeDtypeStruct((2, NL, NLON), bf16),
        cost_estimate=pl.CostEstimate(flops=6 * NL * NLON, bytes_accessed=8 * NL * NLON, transcendentals=0),
        compiler_params=params,
        name="harmonics",
    )(coarse_cos, coarse_sin, fine_cos, fine_sin)

    tendency = pl.pallas_call(
        functools.partial(longitude_kernel, width),
        in_specs=[vmem] * 2,
        out_specs=vmem,
        out_shape=jax.ShapeDtypeStruct((NL, 6 * width), bf16),
        scratch_shapes=[pltpu.VMEM((NL, 6 * width), f32)],
        compiler_params=params,
        name="longitude",
    )(pieces, table)
    pieces = lax.all_to_all(
        tendency.reshape(members, slots, 6 * width), "ma", split_axis=0, concat_axis=0, tiled=True
    ).reshape(members * slots, 6 * width)

    lanes = 6 * slots * radii
    sides = pl.pallas_call(
        functools.partial(analysis_kernel, groups, width),
        in_specs=[vmem] * 3,
        out_specs=vmem,
        out_shape=jax.ShapeDtypeStruct((NL, lanes), bf16),
        scratch_shapes=[
            pltpu.VMEM((pl.cdiv(6 * width, LANES), members * slots, LANES), f32),
            pltpu.VMEM((NL // LANES, lanes, LANES), f32),
        ],
        compiler_params=params,
        name="analysis",
    )(pieces, velocity_rows, weighted_rows)
    columns = lax.all_to_all(
        sides.reshape(owners, degrees, lanes), "row", split_axis=0, concat_axis=0, tiled=True
    ).reshape(NL, lanes)

    advanced = pl.pallas_call(
        solve_kernel,
        in_specs=[vmem] * 2,
        out_specs=vmem,
        out_shape=jax.ShapeDtypeStruct((6 * slots * degrees, NR), f32),
        scratch_shapes=[
            pltpu.VMEM((lanes // LANES, NL, LANES), f32),
            pltpu.VMEM((degrees, NR, LANES), f32),
        ],
        compiler_params=params,
        name="solve",
    )(columns, inverse_operators)
    return advanced.reshape(3, 2, slots, degrees, NR)


def solution(mesh):
    in_specs = (
        P(None, None, "ma", "row", None),
        P(None, None, "ma", "row", None),
        P(),
        P("ma", None, None),
        P("ma", None, None),
        P("row", None, None),
    )
    out_specs = P(None, None, "ma", "row", None)
    return jax.shard_map(
        per_device, mesh=mesh, in_specs=in_specs, out_specs=out_specs, check_vma=False
    )
```

time: 136 us -> 128 us (0.941)
  Pallas kernels: 26.3 us -> 17.5 us
  waiting for transfers between devices: 28.7 us -> 32.1 us
    pallas_call x1, Pallas kernels: 5.79 us -> 1.19 us  [per_device(): pl.pallas_call(functools.partial(analysis_kernel, groups, width), in_spec...]
    all_to_all x1, waiting for transfers between devices: 28.7 us -> 32.1 us  [per_device(): lax.all_to_all(sums.reshape(members, slots, 12 * width), 'ma', split_axis...]
    pallas_call x1, Pallas kernels: 5.39 us -> 2.85 us  [per_device(): pl.pallas_call(functools.partial(longitude_kernel, width), in_specs=[vmem...]
    pallas_call x1, Pallas kernels: 3.51 us -> 1.05 us  [per_device(): pl.pallas_call(harmonics_kernel, in_specs=[vmem] * 4, out_specs=vmem, out...]
  transfers between devices with their start and end apart: 1 -> 1, of which waited for: 1 -> 1; matrix products, arithmetic and copies ran while one was open for 2% -> 1% of each run, Pallas kernels for 3% -> 1%
where the time goes in v2:
time: 128 us; the launch traced here: 127 us
  blocking collectives  58.2 us (45%)
  waiting for transfers between devices  32.1 us (25%)
  Pallas kernels  17.5 us (14%)
  starting transfers between devices  16.4 us (13%)
  other arithmetic  1.67 us (1%)
  local copies, waits for them, and re-layouts  1.35 us (1%)
    all_to_all x1, waiting for transfers between devices, per_device(): lax.all_to_all(sums.reshape(members, slots, 12 * width), 'ma', split_axis...  32.1 us
    all_to_all x1, blocking collectives, per_device(): lax.all_to_all(sides.reshape(owners, degrees, lanes), 'row', split_axis=0...  30.9 us
    all_to_all x1, blocking collectives, per_device(): lax.all_to_all(tendency.reshape(members, slots, 6 * width), 'ma', split_a...  27.3 us
    all_to_all x1, starting transfers between devices, per_device(): lax.all_to_all(sums.reshape(members, slots, 12 * width), 'ma', split_axis...  16.4 us
    pallas_call x1, Pallas kernels, per_device(): pl.pallas_call(functools.partial(synthesis_kernel, groups, width), grid=(...  8.83 us
    pallas_call x1, Pallas kernels, per_device(): pl.pallas_call(solve_kernel, in_specs=[vmem] * 2, out_specs=vmem, out_sha...  3.63 us
    pallas_call x1, Pallas kernels, per_device(): pl.pallas_call(functools.partial(longitude_kernel, width), in_specs=[vmem...  2.85 us
  transfers between devices with their start and end apart: 1, of which 1 were waited for; matrix products, arithmetic and copies ran while one was open for 1% of the time, Pallas kernels for 1%

profile of v2, /device:TPU:1, one launch (start us, length us, event | category | flops | bytes accessed | tf_op | source)
XLA Modules:
  0.0 127.4 jit_solution(14675767773684683405)
XLA Ops:
  0.0 0.0 copy-start.3
  0.0 1.3 %dynamic_slice.3.orders = s32[8]{0:T(128)} dynamic-slice(s32[384]{0:T(512)} %param.8, s32[]{:T(128)S(6)} %select_n.24), dynamic_slice_sizes={8} | dynamic-slice | bytes 68 | tf_op jit(solution)/shard_map/dynamic_slice | solution.py:189
  1.3 8.8 %synthesis.1 = bf16[384,1152]{1,0:T(8,128)(2,1)} custom-call(s32[8]{0:T(128)} %dynamic_slice.3.orders, bf16[6,8,8,384]{3,2,1,0:T(8,128)(2,1)} %bitcast.17, bf16[6,8,8,384]{3,2,1,0:T(8,128)(2,1)} %bitcast.21, bf16[8,576,384]{2,1,0:T(8,128)(2,1)} %bitcast.19), custom_call_target="tpu_custom_call" | custom-call | tf_op jit(solution)/shard_map/synthesis/pallas_call | solution.py:196
  10.2 16.4 %all-to-all-start = ((bf16[48,8,1152]{2,1,0:T(8,128)(2,1)}), bf16[48,8,1152]{2,1,0:T(8,128)(2,1)S(1)}, u32[]{:S(2)}, u32[]{:S(2)}) async-start(bf16[48,8,1152]{2,1,0:T(8,128)(2,1)} %bitcast.20), calls=%async_computation | async-start | bytes 1769472 | tf_op jit(solution)/shard_map/all_to_all | solution.py:212
  26.6 0.0 copy-done.3
  26.6 1.7 %fusion.10 = (f32[384,128]{1,0:T(8,128)S(1)}, f32[384,128]{1,0:T(8,128)S(1)}, f32[384,128]{1,0:T(8,128)S(1)}, f32[384,128]{1,0:T(8,128)S(1)}) fusion(s32[128]{0:T(128)S(1)} %and_select_fusion, s32[384]{0:T(512)S(1)} %copy-done.3), kind=kLoop, calls=%fused_computation.14 | loop fusion | flops 884736 | bytes 788480 | tf_op jit(solution)/shard_map/sin | solution.py:31
  28.3 0.0 copy-start.2
  28.3 1.1 harmonics.1.table
  29.3 32.1 %all-to-all-done = bf16[48,8,1152]{2,1,0:T(8,128)(2,1)S(1)} async-done(((bf16[48,8,1152]{2,1,0:T(8,128)(2,1)}), bf16[48,8,1152]{2,1,0:T(8,128)(2,1)S(1)}, u32[]{:S(2)}, u32[]{:S(2)}) %all-to-all-start) | async-done | bytes 884768 | tf_op jit(solution)/shard_map/all_to_all | solution.py:212
  61.4 0.0 copy-start
  61.4 2.8 %longitude.1 = bf16[384,576]{1,0:T(8,128)(2,1)S(1)} custom-call(bf16[384,1152]{1,0:T(8,128)(2,1)S(1)} %bitcast.11, bf16[2,384,1152]{2,1,0:T(8,128)(2,1)S(1)} %harmonics.1.table), custom_call_target="tpu_custom_call" | custom-call | tf_op jit(solution)/shard_map/longitude/pallas_call | solution.py:228
  64.3 0.0 copy-start.1
  64.3 27.3 %all_to_all.15 = bf16[48,8,576]{2,1,0:T(8,128)(2,1)S(1)} all-to-all(bf16[48,8,576]{2,1,0:T(8,128)(2,1)S(1)} %bitcast.13), channel_id=1, replica_groups=mesh['ma'=48,'row'=16] {'ma'}, dimensions={0} | all-to-all | bytes 884736 | tf_op jit(solution)/shard_map/all_to_all | solution.py:237
  91.6 0.0 copy-done.2
  91.6 0.0 copy-done
  91.6 1.2 analysis.1
  92.8 30.9 %all_to_all.16 = bf16[16,24,384]{2,1,0:T(8,128)(2,1)S(1)} all-to-all(bf16[16,24,384]{2,1,0:T(8,128)(2,1)S(1)} %bitcast.15), channel_id=1, replica_groups=mesh['ma'=48,'row'=16] {'row'}, dimensions={0} | all-to-all | bytes 589824 | tf_op jit(solution)/shard_map/all_to_all | solution.py:254
  123.7 0.0 copy-done.1
  123.7 3.6 %solve.1 = f32[1152,128]{1,0:T(8,128)} custom-call(bf16[384,384]{1,0:T(8,128)(2,1)S(1)} %bitcast.16, f32[24,128,128]{2,1,0:T(8,128)S(1)} %copy-done.1), custom_call_target="tpu_custom_call" | custom-call | tf_op jit(solution)/shard_map/solve/pallas_call | solution.py:258
  (1 shorter events, 0.0 us)
Async XLA Ops:
  0.0 26.6 %copy-start.3 = (s32[384]{0:T(512)S(1)}, s32[384]{0:T(512)}, u32[]{:S(2)}) copy-start(s32[384]{0:T(512)} %param.8) | copy-start | bytes 4612
  10.2 51.3 %all-to-all-start = ((bf16[48,8,1152]{2,1,0:T(8,128)(2,1)}), bf16[48,8,1152]{2,1,0:T(8,128)(2,1)S(1)}, u32[]{:S(2)}, u32[]{:S(2)}) async-start(bf16[48,8,1152]{2,1,0:T(8,128)(2,1)} %bitcast.20), calls=%async_computation | async-start | bytes 1769472 | tf_op jit(solution)/shard_map/all_to_all | solution.py:212
  28.3 63.4 %copy-start.2 = (bf16[3,2,8,8,384]{4,3,2,1,0:T(8,128)(2,1)S(1)}, bf16[3,2,8,8,384]{4,3,2,1,0:T(8,128)(2,1)}, u32[]{:S(2)}) copy-start(bf16[3,2,8,8,384]{4,3,2,1,0:T(8,128)(2,1)} %param.6) | copy-start | bytes 884740
  61.4 30.2 %copy-start = (bf16[8,384,576]{1,2,0:T(8,128)(2,1)S(1)}, bf16[8,384,576]{1,2,0:T(8,128)(2,1)}, u32[]{:S(2)}) copy-start(bf16[8,384,576]{1,2,0:T(8,128)(2,1)} %param.10) | copy-start | bytes 10616836
  64.3 59.4 %copy-start.1 = (f32[24,128,128]{2,1,0:T(8,128)S(1)}, f32[24,128,128]{2,1,0:T(8,128)}, u32[]{:S(2)}) copy-start(f32[24,128,128]{2,1,0:T(8,128)} %operators.1) | copy-start | bytes 4718596

commit v3 on v2

--- a/solution.py
+++ b/solution.py
@@ -38,8 +38,8 @@
         cos_a = coarse_cos[:, block : block + 1]
         sin_a = coarse_sin[:, block : block + 1]
         lanes = pl.ds(block * LANES, LANES)
-        table[0, :, lanes] = (cos_a * cos_b - sin_a * sin_b).astype(jnp.bfloat16)
-        table[1, :, lanes] = (-(sin_a * cos_b + cos_a * sin_b)).astype(jnp.bfloat16)
+        table[:NL, lanes] = (cos_a * cos_b - sin_a * sin_b).astype(jnp.bfloat16)
+        table[NL:, lanes] = (-(sin_a * cos_b + cos_a * sin_b)).astype(jnp.bfloat16)
 
 
 def lane_index():
@@ -69,41 +69,57 @@
     return piece
 
 
-def synthesis_kernel(groups, width, orders, velocity, vorticity, legendre, out, stage):
-    slot = pl.program_id(0)
-    slots = orders.shape[0]
-    radii = velocity.shape[1]
-    count = 12 * radii
-    own = jnp.where(orders[slot] == 0, 1.0, 2.0).astype(jnp.float32) / NL
-    spectral = jnp.concatenate([velocity[...], vorticity[...]], axis=0)
-    spectral = spectral.astype(jnp.float32).reshape(count, NL).astype(jnp.bfloat16)
-    rows = pl.ds(pl.multiple_of(slot * count, 8), count)
+def synthesis_kernel(
+    groups, width, orders, velocity, vorticity, legendre, out, fields, tables, stage, turned, field_sems, table_sems
+):
+    slots = tables.shape[0]
+    radii = fields.shape[3]
+    copies = [
+        pltpu.make_async_copy(source, fields.at[index], field_sems.at[index])
+        for index, source in enumerate((velocity, vorticity))
+    ]
+    loads = [
+        pltpu.make_async_copy(legendre.at[slot], tables.at[slot], table_sems.at[slot]) for slot in range(slots)
+    ]
+    for copy in copies + loads:
+        copy.start()
+    for copy in copies:
+        copy.wait()
+    first = lax.axis_index("ma") * slots
+    for slot in range(slots):
+        own = jnp.where(orders[first + slot] == 0, 1.0, 2.0).astype(jnp.float32) / NL
+        spectral = fields[:, :, slot].astype(jnp.float32).reshape(12 * radii, NL).astype(jnp.bfloat16)
+        loads[slot].wait()
+        for group in range(groups):
+            part = dot(spectral, tables[slot, group * width : (group + 1) * width, :], NT_DIMS) * own
+            for field in range(12):
+                stage[field, slot * radii : (slot + 1) * radii, group * LANES : group * LANES + width] = part[
+                    field * radii : (field + 1) * radii
+                ]
+    count = slots * radii
+    row = lax.broadcasted_iota(jnp.int32, (count, count), 0)
+    column = lax.broadcasted_iota(jnp.int32, (count, count), 1)
+    swap = (column == row % slots * radii + row // slots).astype(jnp.float32).astype(jnp.bfloat16)
+    for field in range(12):
+        turned[field] = dot(swap, stage[field].astype(jnp.bfloat16))
     for group in range(groups):
-        part = dot(spectral, legendre[0, group * width : (group + 1) * width, :], NT_DIMS)
-        stage[group, rows, :width] = part * own
-
-    @pl.when(slot == slots - 1)
-    def finish():
-        def receiver(index, carry):
-            group, radius = index // radii, index % radii
+        for radius in range(radii):
             pieces = [
-                stage[group, pl.ds((component * 2 + part) * radii + radius, slots, stride=count), :]
+                turned[component * 2 + part, radius * slots : (radius + 1) * slots, group * LANES : (group + 1) * LANES]
                 for part in range(2)
                 for component in range(6)
             ]
-            target = pl.ds(pl.multiple_of(index * slots, 8), slots)
+            target = (group * radii + radius) * slots
             for tile in range(12 * width // LANES):
-                lanes = slice(tile * LANES, (tile + 1) * LANES)
-                out[target, lanes] = joined(pieces, width, tile).astype(jnp.bfloat16)
-            return carry
-
-        lax.fori_loop(0, groups * radii, receiver, 0, unroll=4)
+                out[target : target + slots, tile * LANES : (tile + 1) * LANES] = joined(pieces, width, tile).astype(
+                    jnp.bfloat16
+                )
 
 
 def longitude_kernel(width, received, table, out, stage):
     points = 6 * width
     turned = received[...].astype(jnp.float32).T.astype(jnp.bfloat16)
-    grid = dot(turned[:points], table[0]) + dot(turned[points:], table[1])
+    grid = dot(jnp.concatenate([turned[:points], turned[points:]], axis=1), table[...])
     u = [grid[c * width : (c + 1) * width] for c in range(3)]
     w = [grid[(3 + c) * width : (4 + c) * width] for c in range(3)]
     spin = w[2] + rotation
@@ -115,9 +131,9 @@
         ],
         axis=0,
     ).astype(jnp.bfloat16)
+    back = (dot(products, table[...], NT_DIMS) * (NL / NLON)).T
     for part in range(2):
-        back = dot(table[part], products, NT_DIMS) * (NL / NLON)
-        stage[:, part * 3 * width : (part + 1) * 3 * width] = back
+        stage[:, part * 3 * width : (part + 1) * 3 * width] = back[part * NL : (part + 1) * NL]
     out[...] = stage[...].astype(jnp.bfloat16)
 
 
@@ -148,30 +164,38 @@
         out[tile * LANES : (tile + 1) * LANES, :] = side[tile].T.astype(jnp.bfloat16)
 
 
-def solve_kernel(received, operators, out, whole, square):
+def operators_kernel(radii, operators, out):
     degrees = operators.shape[0]
-    owners = received.shape[0] // degrees
-    radii = NR // owners
+    owners = NR // radii
+    row = lax.broadcasted_iota(jnp.int32, (NR, NR), 0)
+    column = lax.broadcasted_iota(jnp.int32, (NR, NR), 1)
+    swap = (row == column % owners * radii + column // owners).astype(jnp.float32).astype(jnp.bfloat16)
+    for degree in range(degrees):
+        operator = operators[degree]
+        high = operator.astype(jnp.bfloat16)
+        low = (operator - high.astype(jnp.float32)).astype(jnp.bfloat16)
+        out[degree, :, :NR] = dot(high, swap).astype(jnp.bfloat16)
+        out[degree, :, NR:] = dot(low, swap).astype(jnp.bfloat16)
+
+
+def solve_kernel(radii, received, operators, out, whole, results):
+    degrees = operators.shape[0]
+    owners = NR // radii
     count = received.shape[1] // radii
     tiles = whole.shape[0]
     for tile in range(tiles):
         whole[tile] = received[:, tile * LANES : (tile + 1) * LANES].astype(jnp.float32)
-
-    def solve(degree, carry):
-        for half in range(owners // 8):
-            source = pl.ds(half * 8 * degrees + degree, 8, stride=degrees)
-            parts = [whole[tile, source, :] for tile in range(tiles)]
-            for radius in range(radii):
-                target = pl.ds(half * 8 * radii + radius, 8, stride=radii)
-                square[degree, target, :] = parted(parts, count, radius)
-        columns = square[degree].T[:count].astype(jnp.bfloat16)
-        operator = operators[degree]
-        high = operator.astype(jnp.bfloat16)
-        low = (operator - high.astype(jnp.float32)).astype(jnp.bfloat16)
-        out[pl.ds(degree, count, stride=degrees), :] = dot(columns, high, NT_DIMS) + dot(columns, low, NT_DIMS)
-        return carry
-
-    lax.fori_loop(0, degrees, solve, 0, unroll=4)
+    for degree in range(degrees):
+        halves = [
+            [whole[tile, pl.ds(half * 8 * degrees + degree, 8, stride=degrees), :] for tile in range(tiles)]
+            for half in range(owners // 8)
+        ]
+        pieces = [parted(parts, count, radius) for radius in range(radii) for parts in halves]
+        columns = jnp.concatenate(pieces, axis=0).T[:count].astype(jnp.bfloat16)
+        both = jnp.concatenate([columns, columns], axis=1)
+        results[degree * count : (degree + 1) * count, :] = dot(both, operators[degree], NT_DIMS)
+    for row in range(count):
+        out[row * degrees : (row + 1) * degrees, :] = results[pl.ds(row, degrees, stride=count), :]
 
 
 def per_device(velocity, vorticity, order_table, legendre_bf, weighted, inverse_operators):
@@ -186,29 +210,28 @@
     vmem = pl.BlockSpec(memory_space=pltpu.VMEM)
     params = pltpu.CompilerParams(vmem_limit_bytes=24 * 2**20)
 
-    own_orders = lax.dynamic_slice_in_dim(order_table, lax.axis_index("ma") * slots, slots)
     velocity_rows = velocity.reshape(6, slots, radii, NL)
     vorticity_rows = vorticity.reshape(6, slots, radii, NL)
     legendre_rows = jnp.swapaxes(legendre_bf, 1, 2)
     weighted_rows = jnp.swapaxes(weighted, 1, 2)
 
-    field_spec = pl.BlockSpec((6, None, radii, NL), lambda s: (0, s, 0, 0))
+    hbm = pl.BlockSpec(memory_space=pl.ANY)
     sums = pl.pallas_call(
         functools.partial(synthesis_kernel, groups, width),
-        grid=(slots,),
-        in_specs=[
-            pl.BlockSpec(memory_space=pltpu.SMEM),
-            field_spec,
-            field_spec,
-            pl.BlockSpec((1, NLAT, NL), lambda s: (s, 0, 0)),
-        ],
-        out_specs=pl.BlockSpec((members * slots, 12 * width), lambda s: (0, 0)),
+        in_specs=[pl.BlockSpec(memory_space=pltpu.SMEM), hbm, hbm, hbm],
+        out_specs=vmem,
         out_shape=jax.ShapeDtypeStruct((members * slots, 12 * width), bf16),
         scratch_shapes=[
-            pltpu.VMEM((groups, slots * 12 * radii, LANES), f32),
+            pltpu.VMEM((2, 6, slots, radii, NL), bf16),
+            pltpu.VMEM((slots, NLAT, NL), bf16),
+            pltpu.VMEM((12, slots * radii, groups * LANES), f32),
+            pltpu.VMEM((12, slots * radii, groups * LANES), f32),
+            pltpu.SemaphoreType.DMA((2,)),
+            pltpu.SemaphoreType.DMA((slots,)),
         ],
+        compiler_params=pltpu.CompilerParams(vmem_limit_bytes=60 * 2**20),
         name="synthesis",
-    )(own_orders, velocity_rows, vorticity_rows, legendre_rows)
+    )(order_table, velocity_rows, vorticity_rows, legendre_rows)
     pieces = lax.all_to_all(
         sums.reshape(members, slots, 12 * width), "ma", split_axis=0, concat_axis=0, tiled=True
     ).reshape(members * slots, 12 * width)
@@ -219,11 +242,23 @@
         harmonics_kernel,
         in_specs=[vmem] * 4,
         out_specs=vmem,
-        out_shape=jax.ShapeDtypeStruct((2, NL, NLON), bf16),
+        out_shape=jax.ShapeDtypeStruct((2 * NL, NLON), bf16),
         cost_estimate=pl.CostEstimate(flops=6 * NL * NLON, bytes_accessed=8 * NL * NLON, transcendentals=0),
         compiler_params=params,
         name="harmonics",
     )(coarse_cos, coarse_sin, fine_cos, fine_sin)
+
+    operators = pl.pallas_call(
+        functools.partial(operators_kernel, radii),
+        in_specs=[vmem],
+        out_specs=vmem,
+        out_shape=jax.ShapeDtypeStruct((degrees, NR, 2 * NR), bf16),
+        cost_estimate=pl.CostEstimate(
+            flops=4 * degrees * NR**3, bytes_accessed=8 * degrees * NR * NR, transcendentals=0
+        ),
+        compiler_params=params,
+        name="operators",
+    )(inverse_operators)
 
     tendency = pl.pallas_call(
         functools.partial(longitude_kernel, width),
@@ -256,17 +291,17 @@
     ).reshape(NL, lanes)
 
     advanced = pl.pallas_call(
-        solve_kernel,
+        functools.partial(solve_kernel, radii),
         in_specs=[vmem] * 2,
         out_specs=vmem,
         out_shape=jax.ShapeDtypeStruct((6 * slots * degrees, NR), f32),
         scratch_shapes=[
             pltpu.VMEM((lanes // LANES, NL, LANES), f32),
-            pltpu.VMEM((degrees, NR, LANES), f32),
+            pltpu.VMEM((6 * slots * degrees, NR), f32),
         ],
         compiler_params=params,
         name="solve",
-    )(columns, inverse_operators)
+    )(columns, operators)
     return advanced.reshape(3, 2, slots, degrees, NR)
 
 

time: 128 us -> 123 us (0.961)
  blocking collectives: 58.2 us -> 27.2 us
  starting transfers between devices: 16.4 us -> 33 us
  waiting for transfers between devices: 32.1 us -> 46 us
  Pallas kernels: 17.5 us -> 14.6 us
  local copies, waits for them, and re-layouts: 1.35 us -> 0.02 us
    all_to_all x1 -> x0, blocking collectives: 30.9 us -> none  [per_device(): lax.all_to_all(sides.reshape(owners, degrees, lanes), 'row', split_axis=0...]
    all_to_all x0 -> x1, starting transfers between devices: none -> 16.6 us  [per_device(): lax.all_to_all(sides.reshape(owners, degrees, lanes), 'row', split_axis=0...]
    all_to_all x0 -> x1, waiting for transfers between devices: none -> 13.9 us  [per_device(): lax.all_to_all(sides.reshape(owners, degrees, lanes), 'row', split_axis=0...]
    pallas_call x2 -> x3, Pallas kernels: 12.5 us -> 9.26 us  [the longest x1 6.85 us: per_device(): pl.pallas_call(functools.partial(synthesis_kernel, groups, width), in_spe...]
    dynamic_slice x1 -> x0, local copies, waits for them, and re-layouts: 1.33 us -> none  [per_device(): lax.dynamic_slice_in_dim(order_table, lax.axis_index('ma') * slots, slots)]
  transfers between devices with their start and end apart: 1 -> 2, of which waited for: 1 -> 2; matrix products, arithmetic and copies ran while one was open for 1% -> 1% of each run, Pallas kernels for 1% -> 1%
where the time goes in v3:
time: 123 us
  waiting for transfers between devices  46 us (37%)
  starting transfers between devices  33 us (27%)
  blocking collectives  27.2 us (22%)
  Pallas kernels  14.6 us (12%)
  other arithmetic  1.67 us (1%)
    all_to_all x1, waiting for transfers between devices, per_device(): lax.all_to_all(sums.reshape(members, slots, 12 * width), 'ma', split_axis...  32.1 us
    all_to_all x1, blocking collectives, per_device(): lax.all_to_all(tendency.reshape(members, slots, 6 * width), 'ma', split_a...  27.2 us
    all_to_all x1, starting transfers between devices, per_device(): lax.all_to_all(sides.reshape(owners, degrees, lanes), 'row', split_axis=0...  16.6 us
    all_to_all x1, starting transfers between devices, per_device(): lax.all_to_all(sums.reshape(members, slots, 12 * width), 'ma', split_axis...  16.4 us
    all_to_all x1, waiting for transfers between devices, per_device(): lax.all_to_all(sides.reshape(owners, degrees, lanes), 'row', split_axis=0...  13.9 us
    pallas_call x1, Pallas kernels, per_device(): pl.pallas_call(functools.partial(synthesis_kernel, groups, width), in_spe...  6.85 us
  transfers between devices with their start and end apart: 2, of which 2 were waited for; matrix products, arithmetic and copies ran while one was open for 1% of the time, Pallas kernels for 1%

profile of v3, /device:TPU:1, one launch (start us, length us, event | category | flops | bytes accessed | tf_op | source)
XLA Modules:
  0.0 122.6 jit_solution(875489551518247892)
XLA Ops:
  0.0 6.9 %synthesis.1 = bf16[384,1152]{1,0:T(8,128)(2,1)} custom-call(s32[384]{0:T(512)} %orders.1, bf16[6,8,8,384]{3,2,1,0:T(8,128)(2,1)} %bitcast.15, bf16[6,8,8,384]{3,2,1,0:T(8,128)(2,1)} %bitcast.20, bf16[8,576,384]{2,1,0:T(8,128)(2,1)} %bitcast.18), custom_call_target="tpu_custom_call" | custom-call | tf_op jit(solution)/shard_map/synthesis/pallas_call | solution.py:219
  6.9 0.0 copy-start.3
  6.9 16.4 %all-to-all-start = ((bf16[48,8,1152]{2,1,0:T(8,128)(2,1)}), bf16[48,8,1152]{2,1,0:T(8,128)(2,1)S(1)}, u32[]{:S(2)}, u32[]{:S(2)}) async-start(bf16[48,8,1152]{2,1,0:T(8,128)(2,1)} %bitcast.19), calls=%async_computation | async-start | bytes 1769472 | tf_op jit(solution)/shard_map/all_to_all | solution.py:235
  23.3 0.0 copy-done.3
  23.3 1.7 %fusion.10 = (f32[384,128]{1,0:T(8,128)S(1)}, f32[384,128]{1,0:T(8,128)S(1)}, f32[384,128]{1,0:T(8,128)S(1)}, f32[384,128]{1,0:T(8,128)S(1)}) fusion(s32[128]{0:T(128)S(1)} %and_select_fusion, s32[384]{0:T(512)S(1)} %copy-done.3), kind=kLoop, calls=%fused_computation.14 | loop fusion | flops 884736 | bytes 788480 | tf_op jit(solution)/shard_map/sin | solution.py:31
  25.0 1.1 harmonics.1.table
  26.0 32.1 %all-to-all-done = bf16[48,8,1152]{2,1,0:T(8,128)(2,1)S(1)} async-done(((bf16[48,8,1152]{2,1,0:T(8,128)(2,1)}), bf16[48,8,1152]{2,1,0:T(8,128)(2,1)S(1)}, u32[]{:S(2)}, u32[]{:S(2)}) %all-to-all-start) | async-done | bytes 884768 | tf_op jit(solution)/shard_map/all_to_all | solution.py:235
  58.1 0.0 copy-start
  58.1 0.0 copy-start.2
  58.1 2.4 %longitude.1 = bf16[384,576]{1,0:T(8,128)(2,1)S(1)} custom-call(bf16[384,1152]{1,0:T(8,128)(2,1)S(1)} %bitcast.11, bf16[768,1152]{1,0:T(8,128)(2,1)S(1)} %harmonics.1.table), custom_call_target="tpu_custom_call" | custom-call | tf_op jit(solution)/shard_map/longitude/pallas_call | solution.py:263
  60.6 27.2 %all_to_all.15 = bf16[48,8,576]{2,1,0:T(8,128)(2,1)S(1)} all-to-all(bf16[48,8,576]{2,1,0:T(8,128)(2,1)S(1)} %bitcast.13), channel_id=1, replica_groups=mesh['ma'=48,'row'=16] {'ma'}, dimensions={0} | all-to-all | bytes 884736 | tf_op jit(solution)/shard_map/all_to_all | solution.py:272
  87.8 0.0 copy-done
  87.8 0.0 copy-done.2
  87.8 0.0 copy-start.1
  87.8 1.9 %analysis.1 = bf16[384,384]{1,0:T(8,128)(2,1)} custom-call(bf16[384,576]{1,0:T(8,128)(2,1)S(1)} %bitcast.14, bf16[6,8,8,384]{3,2,1,0:T(8,128)(2,1)S(1)} %bitcast.16, bf16[8,576,384]{2,1,0:T(8,128)(2,1)S(1)} %bitcast.12), custom_call_target="tpu_custom_call" | custom-call | tf_op jit(solution)/shard_map/analysis/pallas_call | solution.py:277
  89.7 16.6 %all-to-all-start.2 = ((bf16[16,24,384]{2,1,0:T(8,128)(2,1)}), bf16[16,24,384]{2,1,0:T(8,128)(2,1)S(1)}, u32[]{:S(2)}, u32[]{:S(2)}) async-start(bf16[16,24,384]{2,1,0:T(8,128)(2,1)} %bitcast.8), calls=%async_computation.2 | async-start | bytes 589824 | tf_op jit(solution)/shard_map/all_to_all | solution.py:289
  106.3 0.0 copy-done.1
  106.3 0.6 operators.2
  106.9 13.9 %all-to-all-done.2 = bf16[16,24,384]{2,1,0:T(8,128)(2,1)S(1)} async-done(((bf16[16,24,384]{2,1,0:T(8,128)(2,1)}), bf16[16,24,384]{2,1,0:T(8,128)(2,1)S(1)}, u32[]{:S(2)}, u32[]{:S(2)}) %all-to-all-start.2) | async-done | bytes 294944 | tf_op jit(solution)/shard_map/all_to_all | solution.py:289
  120.8 1.8 %solve.1 = f32[1152,128]{1,0:T(8,128)} custom-call(bf16[384,384]{1,0:T(8,128)(2,1)S(1)} %bitcast.17, bf16[24,128,256]{2,1,0:T(8,128)(2,1)S(1)} %operators.2), custom_call_target="tpu_custom_call" | custom-call | tf_op jit(solution)/shard_map/solve/pallas_call | solution.py:293
  (1 shorter events, 0.0 us)
Async XLA Ops:
  6.9 16.4 %copy-start.3 = (s32[384]{0:T(512)S(1)}, s32[384]{0:T(512)}, u32[]{:S(2)}) copy-start(s32[384]{0:T(512)} %orders.1) | copy-start | bytes 4612
  6.9 51.3 %all-to-all-start = ((bf16[48,8,1152]{2,1,0:T(8,128)(2,1)}), bf16[48,8,1152]{2,1,0:T(8,128)(2,1)S(1)}, u32[]{:S(2)}, u32[]{:S(2)}) async-start(bf16[48,8,1152]{2,1,0:T(8,128)(2,1)} %bitcast.19), calls=%async_computation | async-start | bytes 1769472 | tf_op jit(solution)/shard_map/all_to_all | solution.py:235
  58.1 29.6 %copy-start = (bf16[8,384,576]{1,2,0:T(8,128)(2,1)S(1)}, bf16[8,384,576]{1,2,0:T(8,128)(2,1)}, u32[]{:S(2)}) copy-start(bf16[8,384,576]{1,2,0:T(8,128)(2,1)} %param.10) | copy-start | bytes 10616836
  58.1 29.6 %copy-start.2 = (bf16[3,2,8,8,384]{4,3,2,1,0:T(8,128)(2,1)S(1)}, bf16[3,2,8,8,384]{4,3,2,1,0:T(8,128)(2,1)}, u32[]{:S(2)}) copy-start(bf16[3,2,8,8,384]{4,3,2,1,0:T(8,128)(2,1)} %param.6) | copy-start | bytes 884740
  87.8 18.5 %copy-start.1 = (f32[24,128,128]{2,1,0:T(8,128)S(1)}, f32[24,128,128]{2,1,0:T(8,128)}, u32[]{:S(2)}) copy-start(f32[24,128,128]{2,1,0:T(8,128)} %operators.3) | copy-start | bytes 4718596
  89.7 31.1 %all-to-all-start.2 = ((bf16[16,24,384]{2,1,0:T(8,128)(2,1)}), bf16[16,24,384]{2,1,0:T(8,128)(2,1)S(1)}, u32[]{:S(2)}, u32[]{:S(2)}) async-start(bf16[16,24,384]{2,1,0:T(8,128)(2,1)} %bitcast.8), calls=%async_computation.2 | async-start | bytes 589824 | tf_op jit(solution)/shard_map/all_to_all | solution.py:289

commit v4 on v3

--- a/solution.py
+++ b/solution.py
@@ -70,7 +70,23 @@
 
 
 def synthesis_kernel(
-    groups, width, orders, velocity, vorticity, legendre, out, fields, tables, stage, turned, field_sems, table_sems
+    groups,
+    width,
+    order_table,
+    velocity,
+    vorticity,
+    legendre,
+    out,
+    orders,
+    fields,
+    tables,
+    stage,
+    turned,
+    blocks,
+    order_sem,
+    field_sems,
+    table_sems,
+    block_sems,
 ):
     slots = tables.shape[0]
     radii = fields.shape[3]
@@ -79,29 +95,41 @@
         for index, source in enumerate((velocity, vorticity))
     ]
     loads = [
-        pltpu.make_async_copy(legendre.at[slot], tables.at[slot], table_sems.at[slot]) for slot in range(slots)
+        pltpu.make_async_copy(legendre.at[slot, pl.ds(0, NLAT // 2)], tables.at[slot], table_sems.at[slot])
+        for slot in range(slots)
     ]
+    copies.append(pltpu.make_async_copy(order_table, orders, order_sem))
     for copy in copies + loads:
         copy.start()
-    for copy in copies:
+    for copy in copies + loads:
         copy.wait()
     first = lax.axis_index("ma") * slots
+    count = 12 * radii
+    even = lax.broadcasted_iota(jnp.int32, (count, NL), 1) % 2 == 0
     for slot in range(slots):
-        own = jnp.where(orders[first + slot] == 0, 1.0, 2.0).astype(jnp.float32) / NL
-        spectral = fields[:, :, slot].astype(jnp.float32).reshape(12 * radii, NL).astype(jnp.bfloat16)
-        loads[slot].wait()
-        for group in range(groups):
-            part = dot(spectral, tables[slot, group * width : (group + 1) * width, :], NT_DIMS) * own
-            for field in range(12):
-                stage[field, slot * radii : (slot + 1) * radii, group * LANES : group * LANES + width] = part[
-                    field * radii : (field + 1) * radii
-                ]
+        order = orders[first + slot]
+        own = jnp.where(order == 0, 1.0, 2.0).astype(jnp.float32) / NL
+        mirrored = jnp.where(order % 2 == 0, own, -own)
+        spectral = fields[:, :, slot].astype(jnp.float32).reshape(count, NL)
+        low = jnp.where(even, spectral, 0.0)
+        both = jnp.concatenate([low, spectral - low], axis=0).astype(jnp.bfloat16)
+        for group in range(groups // 2):
+            sums = dot(both, tables[slot, group * width : (group + 1) * width, :], NT_DIMS)
+            for hemisphere, part in enumerate(
+                ((sums[:count] + sums[count:]) * own, (sums[:count] - sums[count:]) * mirrored)
+            ):
+                lane = (group + hemisphere * groups // 2) * LANES
+                for field in range(12):
+                    stage[field, slot * radii : (slot + 1) * radii, lane : lane + width] = part[
+                        field * radii : (field + 1) * radii
+                    ]
     count = slots * radii
     row = lax.broadcasted_iota(jnp.int32, (count, count), 0)
     column = lax.broadcasted_iota(jnp.int32, (count, count), 1)
     swap = (column == row % slots * radii + row // slots).astype(jnp.float32).astype(jnp.bfloat16)
     for field in range(12):
         turned[field] = dot(swap, stage[field].astype(jnp.bfloat16))
+    stores = []
     for group in range(groups):
         for radius in range(radii):
             pieces = [
@@ -111,9 +139,14 @@
             ]
             target = (group * radii + radius) * slots
             for tile in range(12 * width // LANES):
-                out[target : target + slots, tile * LANES : (tile + 1) * LANES] = joined(pieces, width, tile).astype(
-                    jnp.bfloat16
-                )
+                blocks[target : target + slots, tile * LANES : (tile + 1) * LANES] = joined(
+                    pieces, width, tile
+                ).astype(jnp.bfloat16)
+        rows = pl.ds(group * radii * slots, radii * slots)
+        stores.append(pltpu.make_async_copy(blocks.at[rows], out.at[rows], block_sems.at[group]))
+        stores[-1].start()
+    for copy in stores:
+        copy.wait()
 
 
 def longitude_kernel(width, received, table, out, stage):
@@ -137,22 +170,29 @@
     out[...] = stage[...].astype(jnp.bfloat16)
 
 
-def analysis_kernel(groups, width, received, velocity, weighted, out, whole, side):
+def analysis_kernel(groups, width, orders, received, velocity, weighted, out, whole, side):
     slots = weighted.shape[0]
     radii = velocity.shape[2]
     tiles = whole.shape[0]
     for tile in range(tiles):
         size = min(LANES, 6 * width - tile * LANES)
         whole[tile, :, :size] = received[:, tile * LANES : tile * LANES + size].astype(jnp.float32)
+    first = lax.axis_index("ma") * slots
+    count = 6 * radii
+    degree = lax.broadcasted_iota(jnp.int32, (count, NL), 1)
     for slot in range(slots):
-        terms = None
-        for group in range(groups):
-            source = pl.ds(group * radii * slots + slot, radii, stride=slots)
-            parts = [whole[tile, source, :] for tile in range(tiles)]
-            fields = [parted(parts, width, part * 3 + component) for component in range(3) for part in range(2)]
-            block = jnp.concatenate(fields, axis=0)[:, :width].astype(jnp.bfloat16)
-            term = dot(block, weighted[slot, group * width : (group + 1) * width, :])
-            terms = term if terms is None else terms + term
+        total = None
+        for group in range(groups // 2):
+            fields = []
+            for block in (group, group + groups // 2):
+                source = pl.ds(block * radii * slots + slot, radii, stride=slots)
+                parts = [whole[tile, source, :] for tile in range(tiles)]
+                fields += [parted(parts, width, part * 3 + component) for component in range(3) for part in range(2)]
+            both = jnp.concatenate(fields, axis=0)[:, :width].astype(jnp.bfloat16)
+            term = dot(both, weighted[slot, group * width : (group + 1) * width, :])
+            total = term if total is None else total + term
+        odd = (degree + orders[first + slot]) % 2 == 1
+        terms = total[:count] + jnp.where(odd, -total[count:], total[count:])
         known = velocity[:, slot].astype(jnp.float32).reshape(6 * radii, NL)
         right_side = known + time_step * terms
         for field in range(6):
@@ -218,16 +258,20 @@
     hbm = pl.BlockSpec(memory_space=pl.ANY)
     sums = pl.pallas_call(
         functools.partial(synthesis_kernel, groups, width),
-        in_specs=[pl.BlockSpec(memory_space=pltpu.SMEM), hbm, hbm, hbm],
-        out_specs=vmem,
+        in_specs=[hbm] * 4,
+        out_specs=hbm,
         out_shape=jax.ShapeDtypeStruct((members * slots, 12 * width), bf16),
         scratch_shapes=[
+            pltpu.SMEM((NL,), jnp.int32),
             pltpu.VMEM((2, 6, slots, radii, NL), bf16),
-            pltpu.VMEM((slots, NLAT, NL), bf16),
+            pltpu.VMEM((slots, NLAT // 2, NL), bf16),
             pltpu.VMEM((12, slots * radii, groups * LANES), f32),
             pltpu.VMEM((12, slots * radii, groups * LANES), f32),
+            pltpu.VMEM((members * slots, 12 * width), bf16),
+            pltpu.SemaphoreType.DMA,
             pltpu.SemaphoreType.DMA((2,)),
             pltpu.SemaphoreType.DMA((slots,)),
+            pltpu.SemaphoreType.DMA((groups,)),
         ],
         compiler_params=pltpu.CompilerParams(vmem_limit_bytes=60 * 2**20),
         name="synthesis",
@@ -259,6 +303,7 @@
         compiler_params=params,
         name="operators",
     )(inverse_operators)
+    table, operators = lax.optimization_barrier((table, operators))
 
     tendency = pl.pallas_call(
         functools.partial(longitude_kernel, width),
@@ -276,7 +321,7 @@
     lanes = 6 * slots * radii
     sides = pl.pallas_call(
         functools.partial(analysis_kernel, groups, width),
-        in_specs=[vmem] * 3,
+        in_specs=[pl.BlockSpec(memory_space=pltpu.SMEM)] + [vmem] * 3,
         out_specs=vmem,
         out_shape=jax.ShapeDtypeStruct((NL, lanes), bf16),
         scratch_shapes=[
@@ -285,7 +330,7 @@
         ],
         compiler_params=params,
         name="analysis",
-    )(pieces, velocity_rows, weighted_rows)
+    )(order_table, pieces, velocity_rows, weighted_rows)
     columns = lax.all_to_all(
         sides.reshape(owners, degrees, lanes), "row", split_axis=0, concat_axis=0, tiled=True
     ).reshape(NL, lanes)

time: 123 us -> 122 us (level)
  blocking collectives: 27.2 us -> 58.1 us
  starting transfers between devices: 33 us -> 16.5 us
  waiting for transfers between devices: 46 us -> 31.4 us
    all_to_all x0 -> x1, blocking collectives: none -> 30.9 us  [per_device(): lax.all_to_all(sides.reshape(owners, degrees, lanes), 'row', split_axis=0...]
    all_to_all x1 -> x0, starting transfers between devices: 16.6 us -> none  [per_device(): lax.all_to_all(sides.reshape(owners, degrees, lanes), 'row', split_axis=0...]
    all_to_all x1 -> x0, waiting for transfers between devices: 13.9 us -> none  [per_device(): lax.all_to_all(sides.reshape(owners, degrees, lanes), 'row', split_axis=0...]
    pallas_call x1, Pallas kernels: 6.85 us -> 4.46 us  [per_device(): pl.pallas_call(functools.partial(synthesis_kernel, groups, width), in_spe...]
    pallas_call x1, Pallas kernels: 2.43 us -> 3.79 us  [per_device(): pl.pallas_call(functools.partial(longitude_kernel, width), in_specs=[vmem...]
  transfers between devices with their start and end apart: 2 -> 1, of which waited for: 2 -> 1; matrix products, arithmetic and copies ran while one was open for 1% -> 1% of each run, Pallas kernels for 1% -> 1%
where the time goes in v4:
time: 122 us; the launch traced here: 121 us
  blocking collectives  58.1 us (48%)
  waiting for transfers between devices  31.4 us (26%)
  starting transfers between devices  16.5 us (14%)
  Pallas kernels  13.4 us (11%)
  other arithmetic  1.67 us (1%)
    all_to_all x1, waiting for transfers between devices, per_device(): lax.all_to_all(sums.reshape(members, slots, 12 * width), 'ma', split_axis...  31.4 us
    all_to_all x1, blocking collectives, per_device(): lax.all_to_all(sides.reshape(owners, degrees, lanes), 'row', split_axis=0...  30.9 us
    all_to_all x1, blocking collectives, per_device(): lax.all_to_all(tendency.reshape(members, slots, 6 * width), 'ma', split_a...  27.2 us
    all_to_all x1, starting transfers between devices, per_device(): lax.all_to_all(sums.reshape(members, slots, 12 * width), 'ma', split_axis...  16.5 us
    pallas_call x1, Pallas kernels, per_device(): pl.pallas_call(functools.partial(synthesis_kernel, groups, width), in_spe...  4.46 us
    pallas_call x1, Pallas kernels, per_device(): pl.pallas_call(functools.partial(longitude_kernel, width), in_specs=[vmem...  3.79 us
  transfers between devices with their start and end apart: 1, of which 1 were waited for; matrix products, arithmetic and copies ran while one was open for 1% of the time, Pallas kernels for 1%

profile of v4, /device:TPU:1, one launch (start us, length us, event | category | flops | bytes accessed | tf_op | source)
XLA Modules:
  0.0 121.2 jit_solution(12340433266126711161)
XLA Ops:
  0.0 4.5 %synthesis.1 = bf16[384,1152]{1,0:T(8,128)(2,1)} custom-call(s32[384]{0:T(512)} %orders.1, bf16[6,8,8,384]{3,2,1,0:T(8,128)(2,1)} %bitcast.14, bf16[6,8,8,384]{3,2,1,0:T(8,128)(2,1)} %bitcast.20, bf16[8,576,384]{2,1,0:T(8,128)(2,1)} %bitcast.18), custom_call_target="tpu_custom_call" | custom-call | tf_op jit(solution)/shard_map/synthesis/pallas_call | solution.py:259
  4.5 0.0 copy-start.3
  4.5 16.5 %all-to-all-start = ((bf16[48,8,1152]{2,1,0:T(8,128)(2,1)}), bf16[48,8,1152]{2,1,0:T(8,128)(2,1)}, u32[]{:S(2)}, u32[]{:S(2)}) async-start(bf16[48,8,1152]{2,1,0:T(8,128)(2,1)} %bitcast.19), calls=%async_computation | async-start | bytes 1769472 | tf_op jit(solution)/shard_map/all_to_all | solution.py:279
  21.0 0.0 copy-start.1
  21.0 0.0 copy-done.3
  21.1 1.7 %fusion.10 = (f32[384,128]{1,0:T(8,128)S(1)}, f32[384,128]{1,0:T(8,128)S(1)}, f32[384,128]{1,0:T(8,128)S(1)}, f32[384,128]{1,0:T(8,128)S(1)}) fusion(s32[128]{0:T(128)S(1)} %and_select_fusion, s32[384]{0:T(512)S(1)} %copy-done.3), kind=kLoop, calls=%fused_computation.14 | loop fusion | flops 884736 | bytes 788480 | tf_op jit(solution)/shard_map/sin | solution.py:31
  22.7 1.1 harmonics.1.table
  23.8 0.0 copy-done.1
  23.9 0.6 operators.2
  24.4 31.4 %all-to-all-done = bf16[48,8,1152]{2,1,0:T(8,128)(2,1)} async-done(((bf16[48,8,1152]{2,1,0:T(8,128)(2,1)}), bf16[48,8,1152]{2,1,0:T(8,128)(2,1)}, u32[]{:S(2)}, u32[]{:S(2)}) %all-to-all-start) | async-done | bytes 884768 | tf_op jit(solution)/shard_map/all_to_all | solution.py:279
  55.9 0.0 copy-start
  55.9 0.0 copy-start.2
  55.9 3.8 %longitude.1 = bf16[384,576]{1,0:T(8,128)(2,1)S(1)} custom-call(bf16[384,1152]{1,0:T(8,128)(2,1)} %bitcast.4.received, bf16[768,1152]{1,0:T(8,128)(2,1)S(1)} %harmonics.1.table), custom_call_target="tpu_custom_call" | custom-call | tf_op jit(solution)/shard_map/longitude/pallas_call | solution.py:308
  59.7 27.2 %all_to_all.15 = bf16[48,8,576]{2,1,0:T(8,128)(2,1)S(1)} all-to-all(bf16[48,8,576]{2,1,0:T(8,128)(2,1)S(1)} %bitcast.12), channel_id=1, replica_groups=mesh['ma'=48,'row'=16] {'ma'}, dimensions={0} | all-to-all | bytes 884736 | tf_op jit(solution)/shard_map/all_to_all | solution.py:317
  86.9 0.0 copy-done
  86.9 0.0 copy-done.2
  86.9 1.6 %analysis.1 = bf16[384,384]{1,0:T(8,128)(2,1)S(1)} custom-call(s32[384]{0:T(512)S(1)} %copy-done.3, bf16[384,576]{1,0:T(8,128)(2,1)S(1)} %bitcast.13, bf16[6,8,8,384]{3,2,1,0:T(8,128)(2,1)S(1)} %bitcast.15, bf16[8,576,384]{2,1,0:T(8,128)(2,1)S(1)} %bitcast.11), custom_call_target="tpu_custom_call" | custom-call | tf_op jit(solution)/shard_map/analysis/pallas_call | solution.py:322
  88.5 30.9 %all_to_all.16 = bf16[16,24,384]{2,1,0:T(8,128)(2,1)S(1)} all-to-all(bf16[16,24,384]{2,1,0:T(8,128)(2,1)S(1)} %bitcast.17), channel_id=1, replica_groups=mesh['ma'=48,'row'=16] {'row'}, dimensions={0} | all-to-all | bytes 589824 | tf_op jit(solution)/shard_map/all_to_all | solution.py:334
  119.4 1.8 %solve.1 = f32[1152,128]{1,0:T(8,128)} custom-call(bf16[384,384]{1,0:T(8,128)(2,1)S(1)} %bitcast.16, bf16[24,128,256]{2,1,0:T(8,128)(2,1)S(1)} %operators.2), custom_call_target="tpu_custom_call" | custom-call | tf_op jit(solution)/shard_map/solve/pallas_call | solution.py:338
  (1 shorter events, 0.0 us)
Async XLA Ops:
  4.5 16.6 %copy-start.3 = (s32[384]{0:T(512)S(1)}, s32[384]{0:T(512)}, u32[]{:S(2)}) copy-start(s32[384]{0:T(512)} %orders.1) | copy-start | bytes 4612
  4.5 51.4 %all-to-all-start = ((bf16[48,8,1152]{2,1,0:T(8,128)(2,1)}), bf16[48,8,1152]{2,1,0:T(8,128)(2,1)}, u32[]{:S(2)}, u32[]{:S(2)}) async-start(bf16[48,8,1152]{2,1,0:T(8,128)(2,1)} %bitcast.19), calls=%async_computation | async-start | bytes 1769472 | tf_op jit(solution)/shard_map/all_to_all | solution.py:279
  21.0 2.8 %copy-start.1 = (f32[24,128,128]{2,1,0:T(8,128)S(1)}, f32[24,128,128]{2,1,0:T(8,128)}, u32[]{:S(2)}) copy-start(f32[24,128,128]{2,1,0:T(8,128)} %operators.3) | copy-start | bytes 4718596
  55.9 31.0 %copy-start = (bf16[8,384,576]{1,2,0:T(8,128)(2,1)S(1)}, bf16[8,384,576]{1,2,0:T(8,128)(2,1)}, u32[]{:S(2)}) copy-start(bf16[8,384,576]{1,2,0:T(8,128)(2,1)} %param.10) | copy-start | bytes 10616836
  55.9 31.0 %copy-start.2 = (bf16[3,2,8,8,384]{4,3,2,1,0:T(8,128)(2,1)S(1)}, bf16[3,2,8,8,384]{4,3,2,1,0:T(8,128)(2,1)}, u32[]{:S(2)}) copy-start(bf16[3,2,8,8,384]{4,3,2,1,0:T(8,128)(2,1)} %param.6) | copy-start | bytes 884740

commit v5 on v4

--- a/solution.py
+++ b/solution.py
@@ -31,7 +31,7 @@
     return jnp.cos(angles), jnp.sin(angles)
 
 
-def harmonics_kernel(coarse_cos, coarse_sin, fine_cos, fine_sin, table):
+def tables_kernel(radii, coarse_cos, coarse_sin, fine_cos, fine_sin, operators, table, split):
     cos_b = fine_cos[...]
     sin_b = fine_sin[...]
     for block in range(NLON // LANES):
@@ -40,6 +40,16 @@
         lanes = pl.ds(block * LANES, LANES)
         table[:NL, lanes] = (cos_a * cos_b - sin_a * sin_b).astype(jnp.bfloat16)
         table[NL:, lanes] = (-(sin_a * cos_b + cos_a * sin_b)).astype(jnp.bfloat16)
+    owners = NR // radii
+    row = lax.broadcasted_iota(jnp.int32, (NR, NR), 0)
+    column = lax.broadcasted_iota(jnp.int32, (NR, NR), 1)
+    swap = (row == column % owners * radii + column // owners).astype(jnp.float32).astype(jnp.bfloat16)
+    for degree in range(operators.shape[0]):
+        operator = operators[degree]
+        high = operator.astype(jnp.bfloat16)
+        low = (operator - high.astype(jnp.float32)).astype(jnp.bfloat16)
+        split[degree, :, :NR] = dot(high, swap).astype(jnp.bfloat16)
+        split[degree, :, NR:] = dot(low, swap).astype(jnp.bfloat16)
 
 
 def lane_index():
@@ -204,20 +214,6 @@
         out[tile * LANES : (tile + 1) * LANES, :] = side[tile].T.astype(jnp.bfloat16)
 
 
-def operators_kernel(radii, operators, out):
-    degrees = operators.shape[0]
-    owners = NR // radii
-    row = lax.broadcasted_iota(jnp.int32, (NR, NR), 0)
-    column = lax.broadcasted_iota(jnp.int32, (NR, NR), 1)
-    swap = (row == column % owners * radii + column // owners).astype(jnp.float32).astype(jnp.bfloat16)
-    for degree in range(degrees):
-        operator = operators[degree]
-        high = operator.astype(jnp.bfloat16)
-        low = (operator - high.astype(jnp.float32)).astype(jnp.bfloat16)
-        out[degree, :, :NR] = dot(high, swap).astype(jnp.bfloat16)
-        out[degree, :, NR:] = dot(low, swap).astype(jnp.bfloat16)
-
-
 def solve_kernel(radii, received, operators, out, whole, results):
     degrees = operators.shape[0]
     owners = NR // radii
@@ -282,28 +278,22 @@
 
     coarse_cos, coarse_sin = angle_parts(order_table, LANES * jnp.arange(LANES, dtype=jnp.int32) % NLON)
     fine_cos, fine_sin = angle_parts(order_table, jnp.arange(LANES, dtype=jnp.int32))
-    table = pl.pallas_call(
-        harmonics_kernel,
-        in_specs=[vmem] * 4,
-        out_specs=vmem,
-        out_shape=jax.ShapeDtypeStruct((2 * NL, NLON), bf16),
-        cost_estimate=pl.CostEstimate(flops=6 * NL * NLON, bytes_accessed=8 * NL * NLON, transcendentals=0),
-        compiler_params=params,
-        name="harmonics",
-    )(coarse_cos, coarse_sin, fine_cos, fine_sin)
-
-    operators = pl.pallas_call(
-        functools.partial(operators_kernel, radii),
-        in_specs=[vmem],
-        out_specs=vmem,
-        out_shape=jax.ShapeDtypeStruct((degrees, NR, 2 * NR), bf16),
+    table, operators = pl.pallas_call(
+        functools.partial(tables_kernel, radii),
+        in_specs=[vmem] * 5,
+        out_specs=[vmem] * 2,
+        out_shape=[
+            jax.ShapeDtypeStruct((2 * NL, NLON), bf16),
+            jax.ShapeDtypeStruct((degrees, NR, 2 * NR), bf16),
+        ],
         cost_estimate=pl.CostEstimate(
-            flops=4 * degrees * NR**3, bytes_accessed=8 * degrees * NR * NR, transcendentals=0
+            flops=6 * NL * NLON + 4 * degrees * NR**3,
+            bytes_accessed=8 * NL * NLON + 8 * degrees * NR * NR,
+            transcendentals=0,
         ),
         compiler_params=params,
-        name="operators",
-    )(inverse_operators)
-    table, operators = lax.optimization_barrier((table, operators))
+        name="tables",
+    )(coarse_cos, coarse_sin, fine_cos, fine_sin, inverse_operators)
 
     tendency = pl.pallas_call(
         functools.partial(longitude_kernel, width),

time: 122 us -> 120 us (0.984)
  local copies, waits for them, and re-layouts: 0.02 us -> 2.56 us
  waiting for transfers between devices: 31.4 us -> 29.3 us
  Pallas kernels: 13.4 us -> 11.6 us
    unnamed x8 -> x12, local copies, waits for them, and re-layouts: 0.02 us -> 2.56 us
    all_to_all x1, waiting for transfers between devices: 31.4 us -> 29.3 us  [per_device(): lax.all_to_all(sums.reshape(members, slots, 12 * width), 'ma', split_axis...]
    pallas_call x1, Pallas kernels: 3.79 us -> 2.46 us  [per_device(): pl.pallas_call(functools.partial(longitude_kernel, width), in_specs=[vmem...]
where the time goes in v5:
time: 120 us
  blocking collectives  58.1 us (48%)
  waiting for transfers between devices  29.3 us (24%)
  starting transfers between devices  16.4 us (14%)
  Pallas kernels  11.6 us (10%)
  local copies, waits for them, and re-layouts  2.56 us (2%)
  other arithmetic  1.67 us (1%)
    all_to_all x1, blocking collectives, per_device(): lax.all_to_all(sides.reshape(owners, degrees, lanes), 'row', split_axis=0...  30.9 us
    all_to_all x1, waiting for transfers between devices, per_device(): lax.all_to_all(sums.reshape(members, slots, 12 * width), 'ma', split_axis...  29.3 us
    all_to_all x1, blocking collectives, per_device(): lax.all_to_all(tendency.reshape(members, slots, 6 * width), 'ma', split_a...  27.2 us
    all_to_all x1, starting transfers between devices, per_device(): lax.all_to_all(sums.reshape(members, slots, 12 * width), 'ma', split_axis...  16.4 us
    pallas_call x1, Pallas kernels, per_device(): pl.pallas_call(functools.partial(synthesis_kernel, groups, width), in_spe...  4.43 us
    unnamed x12, local copies, waits for them, and re-layouts  2.56 us
    pallas_call x1, Pallas kernels, per_device(): pl.pallas_call(functools.partial(longitude_kernel, width), in_specs=[vmem...  2.46 us
  transfers between devices with their start and end apart: 1, of which 1 were waited for; matrix products, arithmetic and copies ran while one was open for 1% of the time, Pallas kernels for 1%

profile of v5, /device:TPU:1, one launch (start us, length us, event | category | flops | bytes accessed | tf_op | source)
XLA Modules:
  0.0 119.7 jit_solution(17783026571290459166)
XLA Ops:
  0.0 4.4 %synthesis.1 = bf16[384,1152]{1,0:T(8,128)(2,1)} custom-call(s32[384]{0:T(512)} %orders.1, bf16[6,8,8,384]{3,2,1,0:T(8,128)(2,1)} %bitcast.15, bf16[6,8,8,384]{3,2,1,0:T(8,128)(2,1)} %bitcast.21, bf16[8,576,384]{2,1,0:T(8,128)(2,1)} %bitcast.19), custom_call_target="tpu_custom_call" | custom-call | tf_op jit(solution)/shard_map/synthesis/pallas_call | solution.py:255
  4.4 0.0 copy-start.5
  4.5 16.4 %all-to-all-start = ((bf16[48,8,1152]{2,1,0:T(8,128)(2,1)}), bf16[48,8,1152]{2,1,0:T(8,128)(2,1)S(1)}, u32[]{:S(2)}, u32[]{:S(2)}) async-start(bf16[48,8,1152]{2,1,0:T(8,128)(2,1)} %bitcast.20), calls=%async_computation | async-start | bytes 1769472 | tf_op jit(solution)/shard_map/all_to_all | solution.py:275
  20.9 0.0 copy-done.5
  20.9 1.7 %fusion.10 = (f32[384,128]{1,0:T(8,128)S(1)}, f32[384,128]{1,0:T(8,128)S(1)}, f32[384,128]{1,0:T(8,128)S(1)}, f32[384,128]{1,0:T(8,128)S(1)}) fusion(s32[128]{0:T(128)S(1)} %and_select_fusion, s32[384]{0:T(512)S(1)} %copy-done.5), kind=kLoop, calls=%fused_computation.14 | loop fusion | flops 884736 | bytes 788480 | tf_op jit(solution)/shard_map/sin | solution.py:31
  22.6 0.0 copy-start.1
  22.6 1.4 %copy-done.1 = f32[24,128,128]{2,1,0:T(8,128)S(1)} copy-done((f32[24,128,128]{2,1,0:T(8,128)S(1)}, f32[24,128,128]{2,1,0:T(8,128)}, u32[]{:S(2)}) %copy-start.1) | copy-done | bytes 1572888
  24.0 1.3 %tables.1 = (bf16[768,1152]{1,0:T(8,128)(2,1)S(1)}, bf16[24,128,256]{2,1,0:T(8,128)(2,1)S(1)}) custom-call(f32[384,128]{1,0:T(8,128)S(1)} %get-tuple-element.10.coarse_cos, f32[384,128]{1,0:T(8,128)S(1)} %get-tuple-element.9.coarse_sin, f32[384,128]{1,0:T(8,128)S(1)} %get-tuple-element.12.fine_cos, f32[384,128]{1,0:T(8,128)S(1)} %get-tuple-element.11.fine_sin, ...), custom_call_target="tpu_custom_call" | custom-call | flops 203980800 | bytes 6684672 | tf_op jit(solution)/shard_map/tables/pallas_call | solution.py:281
  25.3 0.0 copy-start.2
  25.3 1.1 copy-done.2
  26.4 29.3 %all-to-all-done = bf16[48,8,1152]{2,1,0:T(8,128)(2,1)S(1)} async-done(((bf16[48,8,1152]{2,1,0:T(8,128)(2,1)}), bf16[48,8,1152]{2,1,0:T(8,128)(2,1)S(1)}, u32[]{:S(2)}, u32[]{:S(2)}) %all-to-all-start) | async-done | bytes 884768 | tf_op jit(solution)/shard_map/all_to_all | solution.py:275
  55.7 0.0 copy-start
  55.7 0.0 copy-start.4
  55.7 2.5 %longitude.1 = bf16[384,576]{1,0:T(8,128)(2,1)S(1)} custom-call(bf16[384,1152]{1,0:T(8,128)(2,1)S(1)} %bitcast.11, bf16[768,1152]{1,0:T(8,128)(2,1)S(1)} %get-tuple-element.7.table), custom_call_target="tpu_custom_call" | custom-call | tf_op jit(solution)/shard_map/longitude/pallas_call | solution.py:298
  58.2 27.2 %all_to_all.15 = bf16[48,8,576]{2,1,0:T(8,128)(2,1)S(1)} all-to-all(bf16[48,8,576]{2,1,0:T(8,128)(2,1)S(1)} %bitcast.13), channel_id=1, replica_groups=mesh['ma'=48,'row'=16] {'ma'}, dimensions={0} | all-to-all | bytes 884736 | tf_op jit(solution)/shard_map/all_to_all | solution.py:307
  85.4 0.0 copy-done
  85.4 0.0 copy-done.4
  85.4 0.0 copy-start.3
  85.4 1.6 %analysis.1 = bf16[384,384]{1,0:T(8,128)(2,1)S(1)} custom-call(s32[384]{0:T(512)S(1)} %copy-done.5, bf16[384,576]{1,0:T(8,128)(2,1)S(1)} %bitcast.14, bf16[6,8,8,384]{3,2,1,0:T(8,128)(2,1)S(1)} %bitcast.16, bf16[8,576,384]{2,1,0:T(8,128)(2,1)S(1)} %bitcast.12), custom_call_target="tpu_custom_call" | custom-call | tf_op jit(solution)/shard_map/analysis/pallas_call | solution.py:312
  87.0 30.9 %all_to_all.16 = bf16[16,24,384]{2,1,0:T(8,128)(2,1)S(1)} all-to-all(bf16[16,24,384]{2,1,0:T(8,128)(2,1)S(1)} %bitcast.18), channel_id=1, replica_groups=mesh['ma'=48,'row'=16] {'row'}, dimensions={0} | all-to-all | bytes 589824 | tf_op jit(solution)/shard_map/all_to_all | solution.py:324
  117.9 0.0 copy-done.3
  117.9 1.8 %solve.1 = f32[1152,128]{1,0:T(8,128)} custom-call(bf16[384,384]{1,0:T(8,128)(2,1)S(1)} %bitcast.17, bf16[24,128,256]{2,1,0:T(8,128)(2,1)S(1)} %copy-done.3), custom_call_target="tpu_custom_call" | custom-call | tf_op jit(solution)/shard_map/solve/pallas_call | solution.py:328
  (1 shorter events, 0.0 us)
Async XLA Ops:
  4.4 16.5 %copy-start.5 = (s32[384]{0:T(512)S(1)}, s32[384]{0:T(512)}, u32[]{:S(2)}) copy-start(s32[384]{0:T(512)} %orders.1) | copy-start | bytes 4612
  4.5 51.3 %all-to-all-start = ((bf16[48,8,1152]{2,1,0:T(8,128)(2,1)}), bf16[48,8,1152]{2,1,0:T(8,128)(2,1)S(1)}, u32[]{:S(2)}, u32[]{:S(2)}) async-start(bf16[48,8,1152]{2,1,0:T(8,128)(2,1)} %bitcast.20), calls=%async_computation | async-start | bytes 1769472 | tf_op jit(solution)/shard_map/all_to_all | solution.py:275
  22.6 1.4 %copy-start.1 = (f32[24,128,128]{2,1,0:T(8,128)S(1)}, f32[24,128,128]{2,1,0:T(8,128)}, u32[]{:S(2)}) copy-start(f32[24,128,128]{2,1,0:T(8,128)} %operators.1) | copy-start | bytes 4718596
  25.3 1.1 copy-start.2
  55.7 29.7 %copy-start = (bf16[8,384,576]{1,2,0:T(8,128)(2,1)S(1)}, bf16[8,384,576]{1,2,0:T(8,128)(2,1)}, u32[]{:S(2)}) copy-start(bf16[8,384,576]{1,2,0:T(8,128)(2,1)} %param.10) | copy-start | bytes 10616836
  55.7 29.7 %copy-start.4 = (bf16[3,2,8,8,384]{4,3,2,1,0:T(8,128)(2,1)S(1)}, bf16[3,2,8,8,384]{4,3,2,1,0:T(8,128)(2,1)}, u32[]{:S(2)}) copy-start(bf16[3,2,8,8,384]{4,3,2,1,0:T(8,128)(2,1)} %param.6) | copy-start | bytes 884740
  85.4 32.5 %copy-start.3 = (bf16[24,128,256]{2,1,0:T(8,128)(2,1)S(1)}, bf16[24,128,256]{2,1,0:T(8,128)(2,1)}, u32[]{:S(2)}) copy-start(bf16[24,128,256]{2,1,0:T(8,128)(2,1)} %copy-done.2) | copy-start | bytes 4718596

commit v6 on v5

--- a/solution.py
+++ b/solution.py
@@ -180,16 +180,14 @@
     out[...] = stage[...].astype(jnp.bfloat16)
 
 
-def analysis_kernel(groups, width, orders, received, velocity, weighted, out, whole, side):
+def analysis_kernel(groups, width, signs, received, velocity, weighted, out, whole, side):
     slots = weighted.shape[0]
     radii = velocity.shape[2]
     tiles = whole.shape[0]
     for tile in range(tiles):
         size = min(LANES, 6 * width - tile * LANES)
         whole[tile, :, :size] = received[:, tile * LANES : tile * LANES + size].astype(jnp.float32)
-    first = lax.axis_index("ma") * slots
     count = 6 * radii
-    degree = lax.broadcasted_iota(jnp.int32, (count, NL), 1)
     for slot in range(slots):
         total = None
         for group in range(groups // 2):
@@ -201,8 +199,7 @@
             both = jnp.concatenate(fields, axis=0)[:, :width].astype(jnp.bfloat16)
             term = dot(both, weighted[slot, group * width : (group + 1) * width, :])
             total = term if total is None else total + term
-        odd = (degree + orders[first + slot]) % 2 == 1
-        terms = total[:count] + jnp.where(odd, -total[count:], total[count:])
+        terms = total[:count] + total[count:] * signs[slot : slot + 1, :]
         known = velocity[:, slot].astype(jnp.float32).reshape(6 * radii, NL)
         right_side = known + time_step * terms
         for field in range(6):
@@ -295,6 +292,11 @@
         name="tables",
     )(coarse_cos, coarse_sin, fine_cos, fine_sin, inverse_operators)
 
+    own_orders = lax.dynamic_slice_in_dim(order_table, lax.axis_index("ma") * slots, slots)
+    parity = (own_orders[:, None] + jnp.arange(NL, dtype=jnp.int32)[None, :]) % 2
+    signs = (1 - 2 * parity).astype(f32)
+    table, signs = lax.optimization_barrier((table, signs))
+
     tendency = pl.pallas_call(
         functools.partial(longitude_kernel, width),
         in_specs=[vmem] * 2,
@@ -311,7 +313,7 @@
     lanes = 6 * slots * radii
     sides = pl.pallas_call(
         functools.partial(analysis_kernel, groups, width),
-        in_specs=[pl.BlockSpec(memory_space=pltpu.SMEM)] + [vmem] * 3,
+        in_specs=[vmem] * 4,
         out_specs=vmem,
         out_shape=jax.ShapeDtypeStruct((NL, lanes), bf16),
         scratch_shapes=[
@@ -320,7 +322,7 @@
         ],
         compiler_params=params,
         name="analysis",
-    )(order_table, pieces, velocity_rows, weighted_rows)
+    )(signs, pieces, velocity_rows, weighted_rows)
     columns = lax.all_to_all(
         sides.reshape(owners, degrees, lanes), "row", split_axis=0, concat_axis=0, tiled=True
     ).reshape(NL, lanes)

time: 120 us -> 120 us (level)
  transfers between devices with their start and end apart: 1 -> 1, of which waited for: 1 -> 1; matrix products, arithmetic and copies ran while one was open for 1% -> 2% of each run, Pallas kernels for 1% -> 1%
where the time goes in v6:
time: 120 us; the launch traced here: 119 us
  blocking collectives  58.1 us (48%)
  waiting for transfers between devices  29.2 us (24%)
  starting transfers between devices  16.4 us (14%)
  Pallas kernels  11 us (9%)
  local copies, waits for them, and re-layouts  2.64 us (2%)
  other arithmetic  1.75 us (1%)
    all_to_all x1, blocking collectives, per_device(): lax.all_to_all(sides.reshape(owners, degrees, lanes), 'row', split_axis=0...  30.9 us
    all_to_all x1, waiting for transfers between devices, per_device(): lax.all_to_all(sums.reshape(members, slots, 12 * width), 'ma', split_axis...  29.2 us
    all_to_all x1, blocking collectives, per_device(): lax.all_to_all(tendency.reshape(members, slots, 6 * width), 'ma', split_a...  27.2 us
    all_to_all x1, starting transfers between devices, per_device(): lax.all_to_all(sums.reshape(members, slots, 12 * width), 'ma', split_axis...  16.4 us
    pallas_call x1, Pallas kernels, per_device(): pl.pallas_call(functools.partial(synthesis_kernel, groups, width), in_spe...  4.43 us
    unnamed x12, local copies, waits for them, and re-layouts  2.56 us
    pallas_call x1, Pallas kernels, per_device(): pl.pallas_call(functools.partial(longitude_kernel, width), in_specs=[vmem...  2.47 us
  transfers between devices with their start and end apart: 1, of which 1 were waited for; matrix products, arithmetic and copies ran while one was open for 2% of the time, Pallas kernels for 1%

profile of v6, /device:TPU:1, one launch (start us, length us, event | category | flops | bytes accessed | tf_op | source)
XLA Modules:
  0.0 119.1 jit_solution(14582616125224747192)
XLA Ops:
  0.0 4.4 %synthesis.1 = bf16[384,1152]{1,0:T(8,128)(2,1)} custom-call(s32[384]{0:T(512)} %order_table.1, bf16[6,8,8,384]{3,2,1,0:T(8,128)(2,1)} %bitcast.16, bf16[6,8,8,384]{3,2,1,0:T(8,128)(2,1)} %bitcast.21, bf16[8,576,384]{2,1,0:T(8,128)(2,1)} %bitcast.19), custom_call_target="tpu_custom_call" | custom-call | tf_op jit(solution)/shard_map/synthesis/pallas_call | solution.py:252
  4.4 0.0 copy-start.5
  4.5 16.4 %all-to-all-start = ((bf16[48,8,1152]{2,1,0:T(8,128)(2,1)}), bf16[48,8,1152]{2,1,0:T(8,128)(2,1)S(1)}, u32[]{:S(2)}, u32[]{:S(2)}) async-start(bf16[48,8,1152]{2,1,0:T(8,128)(2,1)} %bitcast.20), calls=%async_computation | async-start | bytes 1769472 | tf_op jit(solution)/shard_map/all_to_all | solution.py:272
  20.9 0.0 copy-done.5
  20.9 0.1 dynamic_slice.3
  21.0 1.7 %fusion.10 = (f32[384,128]{1,0:T(8,128)S(1)}, f32[384,128]{1,0:T(8,128)S(1)}, f32[384,128]{1,0:T(8,128)S(1)}, f32[384,128]{1,0:T(8,128)S(1)}) fusion(s32[128]{0:T(128)S(1)} %and_select_fusion, s32[384]{0:T(512)S(1)} %copy-done.5), kind=kLoop, calls=%fused_computation.14 | loop fusion | flops 884736 | bytes 788480 | tf_op jit(solution)/shard_map/sin | solution.py:31
  22.7 0.0 copy-start.1
  22.7 1.4 %copy-done.1 = f32[24,128,128]{2,1,0:T(8,128)S(1)} copy-done((f32[24,128,128]{2,1,0:T(8,128)S(1)}, f32[24,128,128]{2,1,0:T(8,128)}, u32[]{:S(2)}) %copy-start.1) | copy-done | bytes 1572888
  24.1 1.3 %tables.1 = (bf16[768,1152]{1,0:T(8,128)(2,1)S(1)}, bf16[24,128,256]{2,1,0:T(8,128)(2,1)S(1)}) custom-call(f32[384,128]{1,0:T(8,128)S(1)} %get-tuple-element.14.coarse_cos, f32[384,128]{1,0:T(8,128)S(1)} %get-tuple-element.13.coarse_sin, f32[384,128]{1,0:T(8,128)S(1)} %get-tuple-element.16.fine_cos, f32[384,128]{1,0:T(8,128)S(1)} %get-tuple-element.15.fine_sin, ...), custom_call_target="tpu_custom_call" | custom-call | flops 203980800 | bytes 6684672 | tf_op jit(solution)/shard_map/tables/pallas_call | solution.py:278
  25.3 0.0 copy-start.2
  25.3 1.1 copy-done.2
  26.5 0.1 fusion.17.signs
  26.6 29.2 %all-to-all-done = bf16[48,8,1152]{2,1,0:T(8,128)(2,1)S(1)} async-done(((bf16[48,8,1152]{2,1,0:T(8,128)(2,1)}), bf16[48,8,1152]{2,1,0:T(8,128)(2,1)S(1)}, u32[]{:S(2)}, u32[]{:S(2)}) %all-to-all-start) | async-done | bytes 884768 | tf_op jit(solution)/shard_map/all_to_all | solution.py:272
  55.7 0.0 copy-start
  55.7 0.0 copy-start.4
  55.7 2.5 %longitude.1 = bf16[384,576]{1,0:T(8,128)(2,1)S(1)} custom-call(bf16[384,1152]{1,0:T(8,128)(2,1)S(1)} %bitcast.11, bf16[768,1152]{1,0:T(8,128)(2,1)S(1)} %get-tuple-element.11.table), custom_call_target="tpu_custom_call" | custom-call | tf_op jit(solution)/shard_map/longitude/pallas_call | solution.py:300
  58.2 27.2 %all_to_all.15 = bf16[48,8,576]{2,1,0:T(8,128)(2,1)S(1)} all-to-all(bf16[48,8,576]{2,1,0:T(8,128)(2,1)S(1)} %bitcast.13), channel_id=1, replica_groups=mesh['ma'=48,'row'=16] {'ma'}, dimensions={0} | all-to-all | bytes 884736 | tf_op jit(solution)/shard_map/all_to_all | solution.py:309
  85.4 0.0 copy-done
  85.4 0.0 copy-done.4
  85.4 0.0 copy-start.3
  85.4 1.0 analysis.1
  86.4 30.9 %all_to_all.16 = bf16[16,24,384]{2,1,0:T(8,128)(2,1)S(1)} all-to-all(bf16[16,24,384]{2,1,0:T(8,128)(2,1)S(1)} %bitcast.18), channel_id=1, replica_groups=mesh['ma'=48,'row'=16] {'row'}, dimensions={0} | all-to-all | bytes 589824 | tf_op jit(solution)/shard_map/all_to_all | solution.py:326
  117.3 0.0 copy-done.3
  117.3 1.8 %solve.1 = f32[1152,128]{1,0:T(8,128)} custom-call(bf16[384,384]{1,0:T(8,128)(2,1)S(1)} %bitcast.15, bf16[24,128,256]{2,1,0:T(8,128)(2,1)S(1)} %copy-done.3), custom_call_target="tpu_custom_call" | custom-call | tf_op jit(solution)/shard_map/solve/pallas_call | solution.py:330
  (1 shorter events, 0.0 us)
Async XLA Ops:
  4.4 16.5 %copy-start.5 = (s32[384]{0:T(512)S(1)}, s32[384]{0:T(512)}, u32[]{:S(2)}) copy-start(s32[384]{0:T(512)} %order_table.1) | copy-start | bytes 4612
  4.5 51.3 %all-to-all-start = ((bf16[48,8,1152]{2,1,0:T(8,128)(2,1)}), bf16[48,8,1152]{2,1,0:T(8,128)(2,1)S(1)}, u32[]{:S(2)}, u32[]{:S(2)}) async-start(bf16[48,8,1152]{2,1,0:T(8,128)(2,1)} %bitcast.20), calls=%async_computation | async-start | bytes 1769472 | tf_op jit(solution)/shard_map/all_to_all | solution.py:272
  22.7 1.4 %copy-start.1 = (f32[24,128,128]{2,1,0:T(8,128)S(1)}, f32[24,128,128]{2,1,0:T(8,128)}, u32[]{:S(2)}) copy-start(f32[24,128,128]{2,1,0:T(8,128)} %operators.1) | copy-start | bytes 4718596
  25.3 1.1 copy-start.2
  55.7 29.7 %copy-start = (bf16[8,384,576]{1,2,0:T(8,128)(2,1)S(1)}, bf16[8,384,576]{1,2,0:T(8,128)(2,1)}, u32[]{:S(2)}) copy-start(bf16[8,384,576]{1,2,0:T(8,128)(2,1)} %param.10) | copy-start | bytes 10616836
  55.7 29.7 %copy-start.4 = (bf16[3,2,8,8,384]{4,3,2,1,0:T(8,128)(2,1)S(1)}, bf16[3,2,8,8,384]{4,3,2,1,0:T(8,128)(2,1)}, u32[]{:S(2)}) copy-start(bf16[3,2,8,8,384]{4,3,2,1,0:T(8,128)(2,1)} %param.6) | copy-start | bytes 884740
  85.4 31.9 %copy-start.3 = (bf16[24,128,256]{2,1,0:T(8,128)(2,1)S(1)}, bf16[24,128,256]{2,1,0:T(8,128)(2,1)}, u32[]{:S(2)}) copy-start(bf16[24,128,256]{2,1,0:T(8,128)(2,1)} %copy-done.2) | copy-start | bytes 4718596
